TPU v7x, 512 devices: a whole 4x8x8 slice. The times are simulated.
512 devices in a mesh: dp: 16 (over y, core), table: 32 (over x, z).
Axes of the slice: x: 4, y: 8, z: 8, core: 2. Of those that a mesh axis runs over, the one named last changes fastest.
Arguments:
- bag_slots: int32 [262144, 32], P(('dp', 'table')), may hold values from -1 to 3071
- labels: float32 [262144], P(('dp', 'table')), may hold values from 0 to 1
- cold_ids: int32 [512, 32, 32], P(('dp', 'table')), may hold values from 0 to 1023
- cold_count: int32 [512, 32], P(('dp', 'table')), may hold values from 1 to 32, 512 in all within a row
- table: float32 [32768, 256], P('table'), may hold values from -1.8 to 1.8
- adagrad_sum: float32 [32768], P('table'), may hold values from 0.1 to 10
- hot_ids: int32 [2048], P('table'), may hold values from 0 to 1023
- w_in: bfloat16 [256, 4096], replicated, may hold values from -0.375 to 0.375
- w_out: bfloat16 [4096], replicated, may hold values from -0.09375 to 0.09375
Outputs:
- new_table: float32 [32768, 256], P('table')
- new_sum: float32 [32768], P('table')
Inputs may be any that keep to these rules, and one draw needn't show every extreme that they name: `bag_slots`: -1 marks an empty bag entry. `cold_count`: each reader's counts sum to 512.
All inputs are finite; a program needn't handle non-finite values.
Results may differ from a plain program's by a relative error of at most 0.0045.
The roundings to bfloat16 on the way count: a program that leaves them out, or rounds other values in their place, can miss the bound.
Values may be sent and summed in bfloat16 or wider, within the bound.
A program may use at most 64 MiB of HBM per device.

v0:
```python
import jax
import jax.numpy as jnp
from jax import lax
from jax.sharding import PartitionSpec as P

learning_rate = 0.3


def adagrad_step(own_table, own_sum, grad):
    new_sum = own_sum + jnp.mean(grad * grad, axis=1)
    new_table = own_table - learning_rate * grad / jnp.sqrt(new_sum)[:, None]
    return (new_table, new_sum)


def per_device(bag_slots, labels, cold_ids, cold_count, table, adagrad_sum, hot_ids, w_in, w_out):
    owners = lax.axis_size("table")
    hot_dev = hot_ids.shape[0]
    slot_cap = cold_ids.shape[2]
    batch = bag_slots.shape[0]
    width = table.shape[1]
    hot_cols = owners * hot_dev
    vocab_size = owners * (hot_dev + slot_cap)
    table_bf = table.astype(jnp.bfloat16)
    hot_rows = table_bf[hot_ids]
    sample_ids = jnp.broadcast_to(jnp.arange(batch, dtype=jnp.int32)[:, None], bag_slots.shape)
    column_ids = jnp.where(bag_slots < 0, vocab_size, bag_slots)
    incidence = (
        jnp.zeros((batch, vocab_size), jnp.bfloat16)
        .at[sample_ids, column_ids]
        .add(jnp.ones(bag_slots.shape, jnp.bfloat16), mode="drop")
    )
    hot_incidence = incidence[:, :hot_cols]
    cold_incidence = incidence[:, hot_cols:]
    asked_ids = lax.all_to_all(cold_ids[0], "table", split_axis=0, concat_axis=0, tiled=True)
    served = table_bf[asked_ids]
    fetched = lax.all_to_all(served, "table", split_axis=0, concat_axis=0, tiled=True)
    live_mask = jnp.arange(slot_cap, dtype=jnp.int32)[None, :] < cold_count[0][:, None]
    fetched = jnp.where(live_mask[..., None], fetched, jnp.zeros_like(fetched))
    cold_pooled = jnp.dot(
        cold_incidence, fetched.reshape(-1, width), preferred_element_type=jnp.float32
    )
    columns = hot_incidence
    pooled = (
        cold_pooled
        + jnp.dot(
            columns,
            lax.all_gather(hot_rows, "table", axis=0, tiled=True),
            preferred_element_type=jnp.float32,
        )
    ).astype(jnp.bfloat16)
    pre_act = jnp.dot(pooled, w_in, preferred_element_type=jnp.float32)
    hidden = jax.nn.relu(pre_act).astype(jnp.bfloat16)
    logit = jnp.dot(hidden, w_out, preferred_element_type=jnp.float32)
    dlogit = jax.nn.sigmoid(logit) - labels
    dhidden = (dlogit[:, None] * w_out.astype(jnp.float32)[None, :] * (pre_act > 0)).astype(
        jnp.bfloat16
    )
    dpooled = lax.dot_general(
        dhidden, w_in, (((1,), (1,)), ((), ())), preferred_element_type=jnp.float32
    ).astype(jnp.bfloat16)
    columns = hot_incidence
    hot_grad = lax.psum_scatter(
        lax.dot_general(
            columns, dpooled, (((0,), (0,)), ((), ())), preferred_element_type=jnp.float32
        ).astype(jnp.bfloat16),
        "table",
        scatter_dimension=0,
        tiled=True,
    ).astype(jnp.float32)
    cold_term = lax.dot_general(
        cold_incidence, dpooled, (((0,), (0,)), ((), ())), preferred_element_type=jnp.float32
    )
    cold_term = jnp.where(live_mask[..., None], cold_term.reshape(owners, slot_cap, width), 0.0)
    returned = lax.all_to_all(
        cold_term.astype(jnp.bfloat16), "table", split_axis=0, concat_axis=0, tiled=True
    ).astype(cold_term.dtype)
    grad = jnp.zeros(table.shape, jnp.float32).at[hot_ids].add(hot_grad)
    grad = grad.at[asked_ids.reshape(-1)].add(returned.reshape(-1, width))
    total_grad = lax.psum(grad.astype(jnp.bfloat16), "dp").astype(jnp.float32)
    new_table, new_sum = adagrad_step(table, adagrad_sum, total_grad)
    return (new_table, new_sum)


def solution(mesh):
    placed = (
        P(("dp", "table"), None),
        P(("dp", "table")),
        P(("dp", "table"), None, None),
        P(("dp", "table"), None),
        P("table", None),
        P("table"),
        P("table"),
        P(),
        P(),
    )
    return jax.shard_map(
        per_device,
        mesh=mesh,
        in_specs=placed,
        out_specs=(P("table", None), P("table")),
        check_vma=False,
    )
```

profile of v0, /device:TPU:1, one launch (start us, length us, event | category | flops | bytes accessed | tf_op | source)
XLA Modules:
  0.0 546.6 jit_solution(1328954373111065597)
XLA Ops:
  7.2 0.0 copy-start
  7.2 0.0 all-gather.3.cloned.1.call-start
  7.2 1.4 convert_element_type.35
  8.6 0.0 copy-start.5
  8.7 0.0 copy-start.4
  8.7 0.7 compare_select_fusion.4
  9.4 1.3 gather_fusion.1
  10.7 0.0 all-gather.3.cloned.1.call-update
  10.7 22.3 %all_to_all.22 = s32[32,1,32]{2,1,0:T(1,128)S(1)} all-to-all(s32[32,1,32]{2,1,0:T(1,128)} %bitcast.24), channel_id=1, replica_groups=mesh['dp'=16,'table'=32] {'table'}, dimensions={0} | all-to-all | bytes 8192 | tf_op jit(solution)/shard_map/all_to_all | solution.py:34
  33.0 0.1 reshape.131
  33.1 5.0 gather_fusion
  38.1 3.9 all-to-all-start.1
  42.0 0.0 reduce-scatter.2.cloned.1.call-start
  42.1 0.1 multiply_reduce_fusion
  42.2 0.1 and_reduce_fusion
  42.3 0.1 copy.11
  42.5 0.1 reshape.161
  42.6 114.8 %scatter_custom_fusion.2 = bf16[1572864]{0:T(1024)(128)(2,1)} fusion(s32[16384]{0:T(1024)S(1)} %reshape.161, bf16[16384]{0:T(1024)(128)(2,1)S(1)} %broadcast.91, bf16[]{:T(256)} %constant.12.clone.1), kind=kCustom, calls=%fused_computation.17 | custom fusion | flops 16384 | bytes 3145730
  157.4 5.8 %reshape.126 = bf16[512,3072]{1,0:T(8,128)(2,1)} reshape(bf16[1572864]{0:T(1024)(128)(2,1)} %scatter_custom_fusion.2) | data formatting | bytes 6291456 | tf_op jit(solution)/shard_map/scatter-add | solution.py:30
  163.2 0.1 iota_compare_fusion
  163.3 0.0 all-to-all-done.1
  163.3 0.2 broadcast_select_fusion
  163.5 1.7 fusion.28
  165.2 0.0 all-gather.3.cloned.1.call-done
  165.2 7.9 %fusion.19 = f32[512,4096]{1,0:T(8,128)} fusion(bf16[256,4096]{1,0:T(8,128)(2,1)S(1)} %copy-done, f32[512,256]{1,0:T(8,128)S(1)} %fusion.28, bf16[2048,256]{1,0:T(8,128)(2,1)} %all-gather.3.cloned.1.call-done, bf16[512,3072]{1,0:T(8,128)(2,1)} %reshape.126), kind=kOutput, calls=%fused_computation.24 | convolution fusion | flops 1610874880 | bytes 14155776 | tf_op jit(solution)/shard_map/dot_general | solution.py:51
  173.2 4.7 fusion
  177.9 1.0 copy-done.1
  179.0 1.4 fusion.14
  180.4 0.5 copy-done.2
  180.8 1.8 convolution_convert_fusion
  182.6 0.0 reduce-scatter.2.cloned.1.call-update
  182.6 1.7 fusion.26
  184.3 1.0 select_convert_fusion.4
  185.3 9.5 %all-to-all-start.2 = ((bf16[32,32,256]{2,1,0:T(8,128)(2,1)}), bf16[32,32,256]{2,1,0:T(8,128)(2,1)}, u32[]{:S(2)}, u32[]{:S(2)}) async-start(bf16[32,32,256]{2,1,0:T(8,128)(2,1)} %select_convert_fusion.4), calls=%async_computation.3 | async-start | bytes 1048576 | tf_op jit(solution)/shard_map/all_to_all | solution.py:74
  194.8 0.0 all-reduce.2.cloned.1.call-start
  194.9 0.5 broadcast.113
  195.4 0.7 reduce.7
  196.1 0.1 reshape.119
  196.2 207.6 %reduce-scatter.2.cloned.1.call-done = bf16[64,256]{1,0:T(8,128)(2,1)} async-done(((bf16[2048,256]{1,0:T(8,128)(2,1)}), bf16[64,256]{1,0:T(8,128)(2,1)}) %reduce-scatter.2.cloned.1.call-update) | async-done | bytes 32784 | tf_op jit(solution)/shard_map/reduce_scatter | solution.py:62
  403.8 2.1 scatter_custom_fusion
  406.0 0.0 all-to-all-done.2
  406.0 8.6 %scatter_custom_fusion.1 = f32[1024,256]{1,0:T(8,128)} fusion(f32[1024,256]{1,0:T(8,128)} %scatter_custom_fusion, s32[1024]{0:T(1024)S(1)} %bitcast.26, bf16[1024,256]{1,0:T(8,128)(2,1)} %bitcast.10), kind=kCustom, calls=%fused_computation.28 | custom fusion | flops 524288 | bytes 1572864 | tf_op jit(solution)/shard_map/scatter-add | solution.py:78
  414.6 2.1 convert_element_type.44
  416.7 0.0 all-reduce.2.cloned.1.call-update
  416.7 119.2 %all-reduce.2.cloned.1.call-done = bf16[1024,256]{1,0:T(8,128)(2,1)} async-done(((bf16[1024,256]{1,0:T(8,128)(2,1)}), bf16[1024,256]{1,0:T(8,128)(2,1)}) %all-reduce.2.cloned.1.call-update) | async-done | bytes 524304 | tf_op jit(solution)/shard_map/psum | solution.py:79
  535.9 1.3 fusion.23
  537.2 0.6 fusion.36
  537.8 2.2 fusion.22
  (28 shorter events, 0.1 us)
Async XLA Ops:
  7.2 158.1 %copy-start = (bf16[256,4096]{1,0:T(8,128)(2,1)S(1)}, bf16[256,4096]{1,0:T(8,128)(2,1)}, u32[]{:S(2)}) copy-start(bf16[256,4096]{1,0:T(8,128)(2,1)} %param.16) | copy-start | bytes 6291460
  7.2 158.0 %all-gather.3.cloned.1.call-start = ((), (), s32[]{:S(2)}) async-start(), calls=%async_computation.6 | async-start | bytes 1081344 | tf_op jit(solution)/shard_map/all_gather | solution.py:47
  8.6 33.4 %copy-start.5 = (bf16[4096]{0:T(1024)(128)(2,1)S(1)}, bf16[4096]{0:T(1024)(128)(2,1)}, u32[]{:S(2)}) copy-start(bf16[4096]{0:T(1024)(128)(2,1)} %param.17) | copy-start | bytes 24580
  8.7 33.4 %copy-start.4 = (s32[512,32]{0,1:T(8,128)S(1)}, s32[512,32]{0,1:T(8,128)}, u32[]{:S(2)}) copy-start(s32[512,32]{0,1:T(8,128)} %param.9) | copy-start | bytes 196612
  10.7 31.4 %copy-start.8 = (s32[2]{0:T(128)S(1)}, s32[2]{0:T(128)}, u32[]{:S(2)}) copy-start(s32[2]{0:T(128)} %constant.6) | copy-start | bytes 28
  33.0 9.2 %copy-start.9 = (s32[2]{0:T(128)S(1)}, s32[2]{0:T(128)}, u32[]{:S(2)}) copy-start(s32[2]{0:T(128)} %constant.18) | copy-start | bytes 28
  38.1 125.2 %all-to-all-start.1 = ((bf16[32,32,256]{2,1,0:T(8,128)(2,1)}), bf16[32,32,256]{2,1,0:T(8,128)(2,1)S(1)}, u32[]{:S(2)}, u32[]{:S(2)}) async-start(bf16[32,32,256]{2,1,0:T(8,128)(2,1)} %bitcast.4), calls=%async_computation.1 | async-start | bytes 1048576 | tf_op jit(solution)/shard_map/all_to_all | solution.py:36
  42.0 361.8 %reduce-scatter.2.cloned.1.call-start = ((), (), s32[]{:S(2)}) async-start(), calls=%async_computation.4 | async-start | bytes 1081344 | tf_op jit(solution)/shard_map/reduce_scatter | solution.py:62
  157.4 5.8 %copy-start.10 = (s32[1,32]{1,0:T(1,128)S(1)}, s32[1,32]{1,0:T(1,128)}, u32[]{:S(2)}) copy-start(s32[1,32]{1,0:T(1,128)} %param.12) | copy-start | bytes 388
  173.2 4.7 copy-start.7
  173.2 5.8 %copy-start.1 = (f32[512,4096]{1,0:T(8,128)S(1)}, f32[512,4096]{1,0:T(8,128)}, u32[]{:S(2)}) copy-start(f32[512,4096]{1,0:T(8,128)} %fusion.19) | copy-start | bytes 25165828
  178.9 1.9 copy-start.2
  185.3 351.9 %copy-start.6 = (f32[1024]{0:T(1024)S(1)}, f32[1024]{0:T(1024)}, u32[]{:S(2)}) copy-start(f32[1024]{0:T(1024)} %param.14) | copy-start | bytes 12292
  185.3 352.5 %copy-start.3 = (f32[1024,256]{1,0:T(8,128)S(1)}, f32[1024,256]{1,0:T(8,128)}, u32[]{:S(2)}) copy-start(f32[1024,256]{1,0:T(8,128)} %param.13) | copy-start | bytes 3145732
  185.3 220.6 %all-to-all-start.2 = ((bf16[32,32,256]{2,1,0:T(8,128)(2,1)}), bf16[32,32,256]{2,1,0:T(8,128)(2,1)}, u32[]{:S(2)}, u32[]{:S(2)}) async-start(bf16[32,32,256]{2,1,0:T(8,128)(2,1)} %select_convert_fusion.4), calls=%async_computation.3 | async-start | bytes 1048576 | tf_op jit(solution)/shard_map/all_to_all | solution.py:74
  194.8 341.1 %all-reduce.2.cloned.1.call-start = ((), (), s32[]{:S(2)}) async-start(), calls=%async_computation.5 | async-start | bytes 1048576 | tf_op jit(solution)/shard_map/psum | solution.py:79
Sparse Core Ops, SparseCore 0:
  11.2 82.7 all-gather.2
  182.7 221.0 reduce-scatter.1
  416.8 119.0 all-reduce.1
where the time goes:
time: 547 us
  waiting for transfers between devices  327 us (60%)
  other arithmetic  136 us (25%)
  blocking collectives  22.3 us (4%)
  matrix products  19.2 us (4%)
  local copies, waits for them, and re-layouts  14.6 us (3%)
  between operations  14 us (3%)
  starting transfers between devices  13.5 us (2%)
    reduce_scatter x1, waiting for transfers between devices, per_device(): lax.psum_scatter(lax.dot_general(columns, dpooled, (((0,), (0,)), ((), ()...  208 us
    psum x1, waiting for transfers between devices, per_device(): total_grad = lax.psum(grad.astype(jnp.bfloat16), 'dp').astype(jnp.float32)  119 us
    unnamed x4, other arithmetic  115 us
    all_to_all x1, blocking collectives, per_device(): lax.all_to_all(cold_ids[0], 'table', split_axis=0, concat_axis=0, tiled=T...  22.3 us
  transfers between devices with their start and end apart: 5, of which 2 were waited for; matrix products, arithmetic and copies ran while one was open for 25% of the time, Pallas kernels for 0%

commit v1 on v0

v1 whole, which is shorter than its diff:
```python
import functools

import jax
import jax.numpy as jnp
from jax import lax
from jax.experimental import pallas as pl
from jax.experimental.pallas import tpu as pltpu
from jax.sharding import PartitionSpec as P

MESH = pl.DeviceIdType.MESH
learning_rate = 0.3
NX, NZ, NY = 4, 8, 8
bf16, f32, i32 = jnp.bfloat16, jnp.float32, jnp.int32


def remote(src, dst, send_sem, recv_sem, dp, table):
    return pltpu.make_async_remote_copy(
        src_ref=src,
        dst_ref=dst,
        send_sem=send_sem,
        recv_sem=recv_sem,
        device_id=(dp, table),
        device_id_type=MESH,
    )


def peer(k, x, z):
    m = k // NX
    kz = (NZ // 2 + (1 - 2 * (m % 2)) * ((m + 1) // 2)) % NZ
    kx = (k + 1) % NX
    return ((x + kx) % NX) * NZ + (z + kz) % NZ


def place():
    dp, me = lax.axis_index("dp"), lax.axis_index("table")
    y, c = dp // 2, dp % 2
    x, z = me // NZ, me % NZ
    partner = y * 2 + (1 - c)
    return dp, me, y, c, x, z, partner


def fetch_kernel(
    table_ref, hot_ids_ref, ids_ref, hot_ref, fetched_ref, asked_ref,
    tb, oh, served,
    ids_s, ids_r, za_s, za_r, xb_s, xb_r, cc_s, cc_r, f_s, f_r,
):
    n = NX * NZ
    dp, me, y, c, x, z, partner = place()
    barrier = pltpu.get_barrier_semaphore()

    def greet(k, _):
        pl.semaphore_signal(barrier, inc=1, device_id=(dp, peer(k, x, z)), device_id_type=MESH)
        return 0

    lax.fori_loop(0, n - 1, greet, 0)
    pl.semaphore_signal(barrier, inc=1, device_id=(partner, me), device_id_type=MESH)

    rows, width = table_ref.shape
    half = hot_ids_ref.shape[1]
    slots = fetched_ref.shape[1]
    tb[...] = table_ref[...].astype(bf16)
    hot_sel = (hot_ids_ref[c] == lax.broadcasted_iota(i32, (half, rows), 1)).astype(f32).astype(bf16)
    hot_ref[x, z, c] = jnp.dot(hot_sel, tb[...], preferred_element_type=f32).astype(bf16)
    asked_ref[me] = ids_ref[me]
    pl.semaphore_wait(barrier, n)

    def send_ids(k, _):
        p = peer(k, x, z)
        remote(ids_ref.at[p], asked_ref.at[me], ids_s.at[p], ids_r.at[me], dp, p).start()
        return 0

    lax.fori_loop(0, n - 1, send_ids, 0)

    def hot_to_x(zs, xo):
        xt = (x + xo) % NX
        blk = hot_ref.at[x, zs, c]
        remote(blk, blk, xb_s.at[xo, zs], xb_r.at[x, zs], dp, xt * NZ + z).start()

    for zo in range(1, NZ):
        zt = (z + zo) % NZ
        blk = hot_ref.at[x, z, c]
        remote(blk, blk, za_s.at[zo], za_r.at[z], dp, x * NZ + zt).start()
    for xo in range(1, NX):
        hot_to_x(z, xo)

    def forward_x(zo, _):
        zs = (z + zo) % NZ
        blk = hot_ref.at[x, zs, c]
        remote(blk, blk, za_s.at[zo], za_r.at[zs], dp, me).wait_recv()
        for xo in range(1, NX):
            hot_to_x(zs, xo)
        return 0

    lax.fori_loop(1, NZ, forward_x, 0)
    line = hot_ref.at[x, :, c]
    remote(line, line, cc_s.at[x], cc_r.at[x], partner, me).start()

    eye = lax.broadcasted_iota(i32, (slots, 128), 0) == lax.broadcasted_iota(i32, (slots, 128), 1)
    chunk = served.shape[1] // slots

    def serve(ch, _):
        for j in range(chunk):
            k = ch * chunk + j
            p = peer(k, x, z)

            def arrived():
                remote(ids_ref.at[p], asked_ref.at[p], ids_s.at[p], ids_r.at[p], dp, p).wait_recv()

            if j == chunk - 1:
                pl.when(k < n - 1)(arrived)
            else:
                arrived()
            row = asked_ref[p].astype(f32)
            col = jnp.sum(jnp.where(eye, row, 0.0), axis=1, keepdims=True)
            hit = col == lax.broadcasted_iota(i32, (slots, rows), 1).astype(f32)
            oh[pl.ds(j * slots, slots), :] = hit.astype(f32).astype(bf16)
        served[ch] = jnp.dot(oh[...], tb[...], preferred_element_type=f32).astype(bf16)
        for j in range(chunk):
            k = ch * chunk + j
            p = peer(k, x, z)
            block = served.at[ch, pl.ds(j * slots, slots)]

            def send():
                remote(block, fetched_ref.at[me], f_s.at[p], f_r.at[me], dp, p).start()

            def keep():
                fetched_ref[me] = served[ch, pl.ds(j * slots, slots)]

            if j == chunk - 1:
                pl.when(k < n - 1)(send)
                pl.when(k == n - 1)(keep)
            else:
                send()
        return 0

    lax.fori_loop(0, n // chunk, serve, 0)

    def line_to_partner(xo, _):
        xs = (x + xo) % NX

        def landed(zs, _):
            blk = hot_ref.at[xs, zs, c]
            remote(blk, blk, xb_s.at[xo, zs], xb_r.at[xs, zs], dp, me).wait_recv()
            return 0

        lax.fori_loop(0, NZ, landed, 0)
        line = hot_ref.at[xs, :, c]
        remote(line, line, cc_s.at[xs], cc_r.at[xs], partner, me).start()
        return 0

    lax.fori_loop(1, NX, line_to_partner, 0)

    def finish_x(xs, _):
        line = hot_ref.at[xs, :, 1 - c]
        remote(line, line, cc_s.at[xs], cc_r.at[xs], partner, me).wait_recv()
        mine = hot_ref.at[xs, :, c]
        remote(mine, mine, cc_s.at[xs], cc_r.at[xs], partner, me).wait_send()
        return 0

    lax.fori_loop(0, NX, finish_x, 0)

    def finish(k, _):
        p = peer(k, x, z)
        remote(served.at[0, pl.ds(0, slots)], fetched_ref.at[p], f_s.at[p], f_r.at[p], dp, p).wait_recv()
        remote(ids_ref.at[p], asked_ref.at[me], ids_s.at[p], ids_r.at[me], dp, p).wait_send()
        remote(served.at[0, pl.ds(0, slots)], fetched_ref.at[me], f_s.at[p], f_r.at[me], dp, p).wait_send()
        return 0

    lax.fori_loop(0, n - 1, finish, 0)

    def finish_hot(zo, _):
        blk = hot_ref.at[x, z, c]
        zs = (z + zo) % NZ

        @pl.when(zo > 0)
        def _():
            remote(blk, blk, za_s.at[zo], za_r.at[z], dp, me).wait_send()

        for xo in range(1, NX):
            remote(blk, blk, xb_s.at[xo, zs], xb_r.at[x, zs], dp, me).wait_send()
        return 0

    lax.fori_loop(0, NZ, finish_hot, 0)


def fetch(table, hot_ids, ids):
    n = NX * NZ
    rows, width = table.shape
    slots = ids.shape[1]
    half = hot_ids.shape[0] // 2
    chunk = min(8, n)
    ids3 = jnp.pad(ids, ((0, 0), (0, 128 - slots)), constant_values=-1).reshape(n, 1, 128)
    dma = pltpu.SemaphoreType.DMA
    vmem = pl.BlockSpec(memory_space=pltpu.VMEM)
    return pl.pallas_call(
        fetch_kernel,
        name="fetch",
        out_shape=(
            jax.ShapeDtypeStruct((NX, NZ, 2, half, width), bf16),
            jax.ShapeDtypeStruct((n, slots, width), bf16),
            jax.ShapeDtypeStruct((n, 1, 128), i32),
        ),
        in_specs=[vmem] * 3,
        out_specs=(vmem,) * 3,
        scratch_shapes=[
            pltpu.VMEM((rows, width), bf16),
            pltpu.VMEM((chunk * slots, rows), bf16),
            pltpu.VMEM((n // chunk, chunk * slots, width), bf16),
            dma((n,)), dma((n,)),
            dma((NZ,)), dma((NZ,)),
            dma((NX, NZ)), dma((NX, NZ)),
            dma((NX,)), dma((NX,)),
            dma((n,)), dma((n,)),
        ],
        compiler_params=pltpu.CompilerParams(collective_id=0, has_side_effects=True),
    )(table, hot_ids.reshape(2, half, 1), ids3)


def mlp_kernel(
    bag_ref, live_ref, hot_ref, cold_ref, labels_ref, w_in_ref, w_out_ref,
    hot_g_ref, cold_g_ref,
    inc, wm, acc, dpool,
):
    batch, vocab = inc.shape
    hot_cols = hot_ref.shape[0]
    width = hot_ref.shape[1]
    hidden_units = w_in_ref.shape[1]
    tiles = vocab // 128
    hot_tiles = hot_cols // 128
    entries = bag_ref.shape[1]
    bag = entries // 8
    sub = lax.broadcasted_iota(i32, (8, entries), 0)
    own = lax.broadcasted_iota(i32, (8, entries), 1) // bag == sub
    tile_ids = lax.broadcasted_iota(i32, (tiles, 8, entries), 0)
    lane_ids = lax.broadcasted_iota(i32, (128, entries), 0)

    def build(i, _):
        outs = []
        for h in range(2):
            v = bag_ref[pl.ds(2 * i + h, 1), :]
            key = jnp.where(own, v >> 7, -1)
            left = (key[None] == tile_ids).astype(f32).reshape(tiles * 8, entries).astype(bf16)
            right = (lane_ids == (v & 127)).astype(f32).astype(bf16)
            outs.append(
                lax.dot_general(left, right, (((1,), (1,)), ((), ())), preferred_element_type=f32)
            )
        at = pl.ds(pl.multiple_of(16 * i, 16), 16)
        for k in range(tiles):
            t = jnp.concatenate([outs[0][8 * k : 8 * k + 8], outs[1][8 * k : 8 * k + 8]], axis=0)
            if k >= hot_tiles:
                t = t * live_ref[:, pl.ds((k - hot_tiles) * 128, 128)]
            inc[at, pl.ds(k * 128, 128)] = t.astype(bf16)
        return 0

    lax.fori_loop(0, batch // 16, build, 0)

    pooled = (
        jnp.dot(inc[:, pl.ds(0, hot_cols)], hot_ref[...], preferred_element_type=f32)
        + jnp.dot(inc[:, pl.ds(hot_cols, vocab - hot_cols)], cold_ref[...], preferred_element_type=f32)
    ).astype(bf16)
    acc[...] = jnp.zeros_like(acc)
    step = acc.shape[1]

    def forward(j, _):
        at = pl.ds(pl.multiple_of(j * step, step), step)
        pre = jnp.dot(pooled, w_in_ref[:, at], preferred_element_type=f32)
        w = w_out_ref[:, at].astype(f32)
        acc[...] += jnp.maximum(pre, 0.0).astype(bf16).astype(f32) * w
        wm[:, at] = jnp.where(pre > 0, w, 0.0).astype(bf16)
        return 0

    lax.fori_loop(0, hidden_units // step, forward, 0)
    logit = jnp.sum(acc[...], axis=1, keepdims=True)
    dlogit = jax.nn.sigmoid(logit) - labels_ref[...]
    dpool[...] = jnp.zeros_like(dpool)

    def backward(j, _):
        at = pl.ds(pl.multiple_of(j * step, step), step)
        dhidden = (dlogit * wm[:, at].astype(f32)).astype(bf16)
        dpool[...] += lax.dot_general(
            dhidden, w_in_ref[:, at], (((1,), (1,)), ((), ())), preferred_element_type=f32
        )
        return 0

    lax.fori_loop(0, hidden_units // step, backward, 0)
    dpooled = dpool[...].astype(bf16)

    for k in range(vocab // 256):
        g = lax.dot_general(
            inc[:, pl.ds(k * 256, 256)], dpooled, (((0,), (0,)), ((), ())), preferred_element_type=f32
        ).astype(bf16)
        if k * 256 < hot_cols:
            for h in range(2):
                hot_g_ref[h, pl.ds(k * 256, 256), :] = g[:, h * 128 : (h + 1) * 128]
        else:
            cold_g_ref[pl.ds(k * 256 - hot_cols, 256), :] = g


def mlp(bag_slots, live, hot_rows, cold_rows, labels, w_in, w_out):
    batch, bag = bag_slots.shape
    hot_cols, width = hot_rows.shape
    cold_cols = cold_rows.shape[0]
    vmem = pl.BlockSpec(memory_space=pltpu.VMEM)
    return pl.pallas_call(
        mlp_kernel,
        name="mlp",
        out_shape=(
            jax.ShapeDtypeStruct((2, hot_cols, 128), bf16),
            jax.ShapeDtypeStruct((cold_cols, width), bf16),
        ),
        in_specs=[vmem] * 7,
        out_specs=(vmem,) * 2,
        scratch_shapes=[
            pltpu.VMEM((batch, hot_cols + cold_cols), bf16),
            pltpu.VMEM((batch, w_in.shape[1]), bf16),
            pltpu.VMEM((batch, 256), f32),
            pltpu.VMEM((batch, width), f32),
        ],
        compiler_params=pltpu.CompilerParams(vmem_limit_bytes=48 << 20),
    )(
        bag_slots.reshape(batch // 8, 8 * bag),
        live,
        hot_rows,
        cold_rows,
        labels.reshape(batch, 1),
        w_in,
        w_out.reshape(1, -1),
    )


def reduce_kernel(
    hot_g, cold_g, asked_ref, hot_pad_ref, total_ref,
    hcore, hsum, hy, hz, ht, ret, oht, gl, gcore, gsum, gy, hfin,
    hc_s, hc_r, hy_s, hy_r, ht_s, ht_r, c_s, c_r, gc_s, gc_r, gy_s, gy_r, ag_s, ag_r, ac_s, ac_r,
):
    n = NX * NZ
    dp, me, y, c, x, z, partner = place()
    barrier = pltpu.get_barrier_semaphore()

    def dp_of(yy):
        return yy * 2 + c

    def greet(k, _):
        pl.semaphore_signal(barrier, inc=1, device_id=(dp, peer(k, x, z)), device_id_type=MESH)
        return 0

    lax.fori_loop(0, n - 1, greet, 0)

    def greet_y(k, _):
        pl.semaphore_signal(barrier, inc=1, device_id=(dp_of((y + k) % NY), me), device_id_type=MESH)
        return 0

    lax.fori_loop(1, NY, greet_y, 0)
    pl.semaphore_signal(barrier, inc=1, device_id=(partner, me), device_id_type=MESH)
    pl.semaphore_wait(barrier, n - 1 + NY)

    def core_send(k, _):
        yt = (y + k) % NY
        remote(hot_g.at[1 - c, :, yt], hcore.at[yt], hc_s.at[yt], hc_r.at[yt], partner, me).start()
        return 0

    lax.fori_loop(0, NY, core_send, 0)

    def cold_send(k, _):
        p = peer(k, x, z)
        remote(cold_g.at[p], ret.at[me], c_s.at[p], c_r.at[me], dp, p).start()
        return 0

    lax.fori_loop(0, n - 1, cold_send, 0)

    def y_send(k, _):
        yt = (y + k) % NY
        remote(hot_g.at[1 - c, :, yt], hcore.at[yt], hc_s.at[yt], hc_r.at[yt], partner, me).wait_recv()
        hsum[yt] = (hot_g[c, :, yt].astype(f32) + hcore[yt].astype(f32)).astype(bf16)

        @pl.when(k < NY)
        def _():
            remote(hsum.at[yt], hy.at[y], hy_s.at[yt], hy_r.at[y], dp_of(yt), me).start()

        return 0

    lax.fori_loop(1, NY + 1, y_send, 0)
    ret[me] = cold_g[me]

    rows = oht.shape[0]
    slots_all = oht.shape[1]
    for r in range(0, rows, 128):
        ids = lax.broadcasted_iota(i32, (128, slots_all), 0) + r
        oht[pl.ds(r, 128), :] = (ids == asked_ref[...]).astype(f32).astype(bf16)
    hfin[...] = jnp.zeros_like(hfin)

    def y_wait(k, tot):
        ys = (y + k) % NY
        remote(hsum.at[ys], hy.at[ys], hy_s.at[ys], hy_r.at[ys], dp_of(ys), me).wait_recv()
        return 0

    lax.fori_loop(1, NY, y_wait, 0)
    hy[y] = hsum[y]
    tot = hy[0].astype(f32)
    for k in range(1, NY):
        tot = tot + hy[k].astype(f32)
    hz[...] = tot.astype(bf16)

    def t_send(k, _):
        p = peer(k, x, z)
        remote(hz.at[p], ht.at[me], ht_s.at[p], ht_r.at[me], dp, p).start()
        return 0

    lax.fori_loop(0, n - 1, t_send, 0)
    ht[me] = hz[me]

    def cold_wait(k, _):
        p = peer(k, x, z)
        remote(cold_g.at[p], ret.at[p], c_s.at[p], c_r.at[p], dp, p).wait_recv()
        return 0

    lax.fori_loop(0, n - 1, cold_wait, 0)
    width = ret.shape[2]
    back = ret[...].reshape(slots_all, width)

    def t_wait(k, _):
        p = peer(k, x, z)
        remote(hz.at[p], ht.at[p], ht_s.at[p], ht_r.at[p], dp, p).wait_recv()
        return 0

    lax.fori_loop(0, n - 1, t_wait, 0)
    hot_tot = jnp.sum(ht[...].astype(f32), axis=0)
    lanes = lax.broadcasted_iota(i32, (8, width), 1) // 128
    hot_tot = jnp.where(lanes == c, jnp.concatenate([hot_tot, hot_tot], axis=1), 0.0)
    hfin[pl.ds(0, 8), :] = hot_tot
    hot_rows = hfin[...].astype(bf16)
    blk = gl.shape[2]
    hot_ids = hot_pad_ref[y]

    def scatter(b, _):
        at = pl.ds(pl.multiple_of(b * blk, blk), blk)
        hot_sel = (lax.broadcasted_iota(i32, (blk, 128), 0) + b * blk == hot_ids).astype(f32).astype(bf16)
        g = jnp.dot(oht[at, :], back, preferred_element_type=f32)
        g = g + jnp.dot(hot_sel, hot_rows, preferred_element_type=f32)
        return g.astype(bf16)

    for q in range(NY):
        yt = (y + 1 + q) % NY
        gl[1 - c, yt] = scatter((1 - c) * NY + yt, 0)
        remote(gl.at[1 - c, yt], gcore.at[yt], gc_s.at[yt], gc_r.at[yt], partner, me).start()
    for q in range(NY):
        yt = (y + 1 + q) % NY
        gl[c, yt] = scatter(c * NY + yt, 0)
    for q in range(NY):
        yt = (y + 1 + q) % NY
        remote(gl.at[1 - c, yt], gcore.at[yt], gc_s.at[yt], gc_r.at[yt], partner, me).wait_recv()
        gsum[yt] = (gl[c, yt].astype(f32) + gcore[yt].astype(f32)).astype(bf16)
        if q < NY - 1:
            remote(gsum.at[yt], gy.at[y], gy_s.at[yt], gy_r.at[y], dp_of(yt), me).start()

    tot = gsum[y].astype(f32)
    for k in range(1, NY):
        ys = (y + k) % NY
        remote(gsum.at[ys], gy.at[ys], gy_s.at[ys], gy_r.at[ys], dp_of(ys), me).wait_recv()
        tot = tot + gy[ys].astype(f32)
    total_ref[c, y] = tot.astype(bf16)

    mine = total_ref.at[c, y]
    for k in range(1, NY):
        yt = (y + k) % NY
        remote(mine, mine, ag_s.at[yt], ag_r.at[y], dp_of(yt), me).start()
    remote(mine, mine, ac_s.at[y], ac_r.at[y], partner, me).start()

    def forward(k, _):
        ys = (y + k) % NY
        b = total_ref.at[c, ys]
        remote(b, b, ag_s.at[ys], ag_r.at[ys], dp_of(ys), me).wait_recv()
        remote(b, b, ac_s.at[ys], ac_r.at[ys], partner, me).start()
        return 0

    lax.fori_loop(1, NY, forward, 0)

    def finish_core(yt, _):
        b = total_ref.at[1 - c, yt]
        remote(b, b, ac_s.at[yt], ac_r.at[yt], partner, me).wait_recv()
        o = total_ref.at[c, yt]
        remote(o, o, ac_s.at[yt], ac_r.at[yt], partner, me).wait_send()
        remote(hot_g.at[1 - c, :, yt], hcore.at[yt], hc_s.at[yt], hc_r.at[yt], partner, me).wait_send()
        remote(gl.at[1 - c, yt], gcore.at[yt], gc_s.at[yt], gc_r.at[yt], partner, me).wait_send()
        return 0

    lax.fori_loop(0, NY, finish_core, 0)

    def finish_y(k, _):
        yt = (y + k) % NY
        remote(hsum.at[yt], hy.at[y], hy_s.at[yt], hy_r.at[y], dp_of(yt), me).wait_send()
        remote(gsum.at[yt], gy.at[y], gy_s.at[yt], gy_r.at[y], dp_of(yt), me).wait_send()
        remote(mine, mine, ag_s.at[yt], ag_r.at[y], dp_of(yt), me).wait_send()
        return 0

    lax.fori_loop(1, NY, finish_y, 0)

    def finish_t(k, _):
        p = peer(k, x, z)
        remote(cold_g.at[p], ret.at[me], c_s.at[p], c_r.at[me], dp, p).wait_send()
        remote(hz.at[p], ht.at[me], ht_s.at[p], ht_r.at[me], dp, p).wait_send()
        return 0

    lax.fori_loop(0, n - 1, finish_t, 0)


def reduce(hot_g, cold_g, asked, hot_ids, rows):
    n = NX * NZ
    slots, width = cold_g.shape[1:]
    blk = rows // (2 * NY)
    hot_pad = jnp.pad(hot_ids.reshape(NY, 8), ((0, 0), (0, 120)), constant_values=-1).reshape(NY, 1, 128)
    dma = pltpu.SemaphoreType.DMA
    vmem = pl.BlockSpec(memory_space=pltpu.VMEM)
    return pl.pallas_call(
        reduce_kernel,
        name="reduce",
        out_shape=jax.ShapeDtypeStruct((2, NY, blk, width), bf16),
        in_specs=[vmem] * 4,
        out_specs=vmem,
        scratch_shapes=[
            pltpu.VMEM((NY, n, 8, 128), bf16),
            pltpu.VMEM((NY, n, 8, 128), bf16),
            pltpu.VMEM((NY, n, 8, 128), bf16),
            pltpu.VMEM((n, 8, 128), bf16),
            pltpu.VMEM((n, 8, 128), bf16),
            pltpu.VMEM((n, slots, width), bf16),
            pltpu.VMEM((rows, n * slots), bf16),
            pltpu.VMEM((2, NY, blk, width), bf16),
            pltpu.VMEM((NY, blk, width), bf16),
            pltpu.VMEM((NY, blk, width), bf16),
            pltpu.VMEM((NY, blk, width), bf16),
            pltpu.VMEM((128, width), f32),
            dma((NY,)), dma((NY,)),
            dma((NY,)), dma((NY,)),
            dma((n,)), dma((n,)),
            dma((n,)), dma((n,)),
            dma((NY,)), dma((NY,)),
            dma((NY,)), dma((NY,)),
            dma((NY,)), dma((NY,)),
            dma((NY,)), dma((NY,)),
        ],
        compiler_params=pltpu.CompilerParams(
            collective_id=1, has_side_effects=True, vmem_limit_bytes=48 << 20
        ),
    )(hot_g.reshape(2, n, NY, 8, 128), cold_g, asked, hot_pad)


def adagrad_step(own_table, own_sum, grad):
    new_sum = own_sum + jnp.mean(grad * grad, axis=1)
    new_table = own_table - learning_rate * grad / jnp.sqrt(new_sum)[:, None]
    return (new_table, new_sum)


def per_device(bag_slots, labels, cold_ids, cold_count, table, adagrad_sum, hot_ids, w_in, w_out):
    n = NX * NZ
    rows, width = table.shape
    slots = cold_ids.shape[2]
    hot_rows, fetched, asked = fetch(table, hot_ids, cold_ids[0])
    live = (jnp.arange(slots, dtype=i32)[None, :] < cold_count[0][:, None]).astype(f32).reshape(1, n * slots)
    hot_g, cold_g = mlp(
        bag_slots, live, hot_rows.reshape(-1, width), fetched.reshape(-1, width), labels, w_in, w_out
    )
    asked_flat = asked[:, 0, :slots].reshape(1, n * slots)
    total = reduce(hot_g, cold_g.reshape(n, slots, width), asked_flat, hot_ids, rows)
    return adagrad_step(table, adagrad_sum, total.reshape(rows, width).astype(f32))


def solution(mesh):
    placed = (
        P(("dp", "table"), None),
        P(("dp", "table")),
        P(("dp", "table"), None, None),
        P(("dp", "table"), None),
        P("table", None),
        P("table"),
        P("table"),
        P(),
        P(),
    )
    return jax.shard_map(
        per_device,
        mesh=mesh,
        in_specs=placed,
        out_specs=(P("table", None), P("table")),
        check_vma=False,
    )
```

time: 547 us -> 126 us (0.23)
  waiting for transfers between devices: 327 us -> 0 us
  other arithmetic: 136 us -> 3.29 us
  Pallas kernels: 0 us -> 112 us
  blocking collectives: 22.3 us -> 0 us
  matrix products: 19.2 us -> 0 us
  starting transfers between devices: 13.5 us -> 0 us
  between operations: 14 us -> 0.78 us
    reduce_scatter x1 -> x0, waiting for transfers between devices: 208 us -> none  [per_device(): lax.psum_scatter(lax.dot_general(columns, dpooled, (((0,), (0,)), ((), ()...]
    psum x1 -> x0, waiting for transfers between devices: 119 us -> none  [per_device(): total_grad = lax.psum(grad.astype(jnp.bfloat16), 'dp').astype(jnp.float32)]
    unnamed x4 -> x0, other arithmetic: 115 us -> none
    pallas_call x0 -> x3, Pallas kernels: none -> 112 us  [the longest x1 56.9 us: reduce(): pl.pallas_call(reduce_kernel, name='reduce', out_shape=jax.ShapeDtypeStru...]
    all_to_all x1 -> x0, blocking collectives: 22.3 us -> none  [per_device(): lax.all_to_all(cold_ids[0], 'table', split_axis=0, concat_axis=0, tiled=T...]
    dot_general x6 -> x0, matrix products: 19.2 us -> none  [the longest x1 7.93 us: per_device(): pre_act = jnp.dot(pooled, w_in, preferred_element_type=jnp.float32)]
    all_to_all x2 -> x0, starting transfers between devices: 13.4 us -> none  [the longest x1 9.49 us: per_device(): lax.all_to_all(cold_term.astype(jnp.bfloat16), 'table', split_axis=0, con...]
    scatter-add x2 -> x0, other arithmetic: 10.8 us -> none  [the longest x1 8.65 us: per_device(): grad = grad.at[asked_ids.reshape(-1)].add(returned.reshape(-1, width))]
  transfers between devices with their start and end apart: 5 -> 0, of which waited for: 2 -> 0; matrix products, arithmetic and copies ran while one was open for 25% -> 0% of each run, Pallas kernels for 0% -> 0%
where the time goes in v1:
time: 126 us
  Pallas kernels  112 us (89%)
  local copies, waits for them, and re-layouts  9.29 us (7%)
  other arithmetic  3.29 us (3%)
    pallas_call x1, Pallas kernels, reduce(): pl.pallas_call(reduce_kernel, name='reduce', out_shape=jax.ShapeDtypeStru...  56.9 us
    pallas_call x1, Pallas kernels, fetch(): pl.pallas_call(fetch_kernel, name='fetch', out_shape=(jax.ShapeDtypeStruc...  37.1 us
    pallas_call x1, Pallas kernels, mlp(): pl.pallas_call(mlp_kernel, name='mlp', out_shape=(jax.ShapeDtypeStruct((2...  18.4 us
    unnamed x21, local copies, waits for them, and re-layouts  5.08 us

profile of v1, /device:TPU:1, one launch (start us, length us, event | category | flops | bytes accessed | tf_op | source)
XLA Modules:
  0.0 125.7 jit_solution(2564540326406422956)
XLA Ops:
  0.6 0.0 copy-start.9
  0.6 0.0 copy-start.6
  0.7 0.0 copy-start
  0.7 1.6 %reshape.86.hot_ids_ref = s32[2,32,1]{2,1,0:T(8,128)} reshape(s32[64]{0:T(128)} %param.15) | data formatting | bytes 512 | tf_op jit(solution)/shard_map/reshape | solution.py:216
  2.2 1.3 %pad.8 = s32[32,128]{1,0:T(8,128)} pad(s32[32,32]{1,0:T(8,128)} %bitcast.19, s32[]{:T(128)} %constant.1.clone.1), padding=0_0x0_96 | pad | bytes 20484 | tf_op jit(solution)/shard_map/jit(_pad)/pad | solution.py:192
  3.5 37.1 %fetch.1 = (bf16[4,8,2,32,256]{4,3,2,1,0:T(8,128)(2,1)}, bf16[32,32,256]{2,1,0:T(8,128)(2,1)}, s32[32,1,128]{2,1,0:T(1,128)}) custom-call(f32[1024,256]{1,0:T(8,128)} %table_ref.1, s32[2,32,1]{2,1,0:T(8,128)} %reshape.86.hot_ids_ref, s32[32,1,128]{2,1,0:T(1,128)} %bitcast.18), custom_call_target="tpu_custom_call" | custom-call | tf_op jit(solution)/shard_map/fetch/pallas_call | solution.py:195
  40.6 1.0 copy.13
  41.6 0.1 reshape.74.bag_ref
  41.7 0.8 copy.15.labels_ref
  42.5 0.0 copy-start.5
  42.6 0.0 copy-start.8
  42.6 0.0 copy-done.9
  42.6 0.1 fusion.2
  42.6 0.1 reshape.85.live_ref
  42.7 0.0 copy-done.6
  42.8 0.0 copy-done
  42.8 0.0 copy-start.1
  42.8 1.2 copy-done.1
  44.0 0.0 copy-start.2
  44.0 1.0 copy-done.2
  45.0 18.4 %mlp.1 = (bf16[2,2048,128]{2,1,0:T(8,128)(2,1)S(1)}, bf16[1024,256]{1,0:T(8,128)(2,1)S(1)}) custom-call(s32[64,256]{1,0:T(8,128)S(1)} %reshape.74.bag_ref, f32[1,1024]{1,0:T(1,128)S(1)} %reshape.85.live_ref, bf16[2048,256]{1,0:T(8,128)(2,1)S(1)} %bitcast.13, bf16[1024,256]{1,0:T(8,128)(2,1)S(1)} %bitcast.15, f32[512,1]{1,0:T(8,128)S(1)} %copy.15.labels_ref, ...), custom_call_target="tpu_custom_call" | custom-call | tf_op jit(solution)/shard_map/mlp/pallas_call | solution.py:304
  63.4 0.0 copy-start.3
  63.4 0.8 copy-done.3
  64.2 0.0 copy-start.7
  64.2 0.0 copy-done.5
  64.3 0.1 reshape_squeeze.3.asked_ref
  64.3 0.0 copy-done.8
  64.3 0.1 reshape.83
  64.4 0.0 copy-start.4
  64.4 1.0 copy-done.4
  65.5 56.9 %reduce.6 = bf16[2,8,64,256]{3,2,1,0:T(8,128)(2,1)S(1)} custom-call(bf16[2,32,8,8,128]{4,3,2,1,0:T(8,128)(2,1)S(1)} %bitcast.14, bf16[32,32,256]{2,1,0:T(8,128)(2,1)S(1)} %bitcast.16, s32[1,1024]{1,0:T(1,128)S(1)} %reshape_squeeze.3.asked_ref, s32[8,1,128]{2,1,0:T(1,128)S(1)} %bitcast.17), custom_call_target="tpu_custom_call" | custom-call | tf_op jit(solution)/shard_map/reduce/pallas_call | solution.py:514
  122.4 0.2 fusion
  122.6 0.1 div.18
  122.7 0.0 copy-done.7
  122.7 0.6 fusion.3
  123.3 2.4 %fusion.1 = f32[1024,256]{1,0:T(8,128)} fusion(f32[1024,256]{1,0:T(8,128)} %table_ref.1, f32[2,8,64,256]{3,2,1,0:T(8,128)S(1)} %get-tuple-element.15, f32[1024]{0:T(1024)S(1)} %get-tuple-element.12), kind=kLoop, calls=%fused_computation.4 | loop fusion | flops 524288 | bytes 3149824 | tf_op jit(solution)/shard_map/sub | solution.py:550
  (4 shorter events, 0.1 us)
Async XLA Ops:
  0.6 41.9 %copy-start.9 = (s32[1,32]{1,0:T(1,128)S(1)}, s32[1,32]{1,0:T(1,128)}, u32[]{:S(2)}) copy-start(s32[1,32]{1,0:T(1,128)} %param.12) | copy-start | bytes 388
  0.6 42.1 %copy-start.6 = (bf16[4096]{0:T(1024)(128)(2,1)S(1)}, bf16[4096]{0:T(1024)(128)(2,1)}, u32[]{:S(2)}) copy-start(bf16[4096]{0:T(1024)(128)(2,1)} %param.17) | copy-start | bytes 24580
  0.7 42.1 %copy-start = (bf16[256,4096]{1,0:T(8,128)(2,1)S(1)}, bf16[256,4096]{1,0:T(8,128)(2,1)}, u32[]{:S(2)}) copy-start(bf16[256,4096]{1,0:T(8,128)(2,1)} %w_in_ref.1) | copy-start | bytes 6291460
  42.5 21.7 %copy-start.5 = (s32[32,1,128]{2,1,0:T(1,128)S(1)}, s32[32,1,128]{2,1,0:T(1,128)}, u32[]{:S(2)}) copy-start(s32[32,1,128]{2,1,0:T(1,128)} %get-tuple-element.11) | copy-start | bytes 49156
  42.6 21.8 %copy-start.8 = (s32[64]{0:T(128)S(1)}, s32[64]{0:T(128)}, u32[]{:S(2)}) copy-start(s32[64]{0:T(128)} %param.15) | copy-start | bytes 772
  42.8 1.2 copy-start.1
  44.0 1.0 copy-start.2
  63.4 0.8 copy-start.3
  64.2 58.5 %copy-start.7 = (f32[1024]{0:T(1024)S(1)}, f32[1024]{0:T(1024)}, u32[]{:S(2)}) copy-start(f32[1024]{0:T(1024)} %param.14) | copy-start | bytes 12292
  64.4 1.0 copy-start.4

commit v2 on v0

v2 whole, which is shorter than its diff:
```python
import functools

import jax
import jax.numpy as jnp
from jax import lax
from jax.experimental import pallas as pl
from jax.experimental.pallas import tpu as pltpu
from jax.sharding import PartitionSpec as P

MESH = pl.DeviceIdType.MESH
learning_rate = 0.3
NX, NZ, NY = 4, 8, 8
bf16, f32, i32 = jnp.bfloat16, jnp.float32, jnp.int32


def remote(src, dst, send_sem, recv_sem, dp, table):
    return pltpu.make_async_remote_copy(
        src_ref=src,
        dst_ref=dst,
        send_sem=send_sem,
        recv_sem=recv_sem,
        device_id=(dp, table),
        device_id_type=MESH,
    )


def peer(k, x, z):
    m = k // NX
    kz = (NZ // 2 + (1 - 2 * (m % 2)) * ((m + 1) // 2)) % NZ
    kx = (k + 1) % NX
    return ((x + kx) % NX) * NZ + (z + kz) % NZ


def place():
    dp, me = lax.axis_index("dp"), lax.axis_index("table")
    y, c = dp // 2, dp % 2
    x, z = me // NZ, me % NZ
    partner = y * 2 + (1 - c)
    return dp, me, y, c, x, z, partner


def step_kernel(
    pre, mid,
    bag_ref, labels_ref, ids_ref, count_ref, table_hbm, sum_ref, hot_ids_ref, w_hbm, w_out_ref,
    table_out, sum_out,
    table_v, w_v, tb, ids3, asked, flat, hot_pad, bag_rows, bag2, sum_col,
    hot, fetched, oh, served, inc, wm, acc, dpool,
    hot_g, cold_g, hcore, hsum, hy, hz, ht, ret, oht, gacc, hfin, gl, gcore, gsum, gy, total,
    in_s, ids_s, ids_r, za_s, za_r, xb_s, xb_r, cc_s, cc_r, f_s, f_r,
    hc_s, hc_r, hy_s, hy_r, ht_s, ht_r, c_s, c_r, gc_s, gc_r, gy_s, gy_r, ag_s, ag_r, ac_s, ac_r,
):
    n = NX * NZ
    dp, me, y, c, x, z, partner = place()
    rows, width = table_v.shape
    slots = fetched.shape[1]
    half = hot.shape[3]
    hot_dev = 2 * half
    hot_cols = n * hot_dev
    per_y = hz.shape[1]
    batch, vocab = inc.shape
    parts = hc_s.shape[0]
    blk = gl.shape[2]

    def dp_of(yy):
        return yy * 2 + c

    def over(lo, hi, body):
        def run(k, _):
            body(k)
            return 0

        lax.fori_loop(lo, hi, run, 0)

    def eye(a, b, shift=0):
        return lax.broadcasted_iota(i32, (a, b), 0) + shift == lax.broadcasted_iota(i32, (a, b), 1)

    def to_column(mask, row):
        return jnp.sum(jnp.where(mask, row, 0.0), axis=1, keepdims=True)

    barrier = pltpu.get_barrier_semaphore()
    over(0, n - 1, lambda k: pl.semaphore_signal(
        barrier, inc=1, device_id=(dp, peer(k, x, z)), device_id_type=MESH))
    over(1, NY, lambda k: pl.semaphore_signal(
        barrier, inc=1, device_id=(dp_of((y + k) % NY), me), device_id_type=MESH))
    pl.semaphore_signal(barrier, inc=1, device_id=(partner, me), device_id_type=MESH)

    load_table = pltpu.make_async_copy(table_hbm, table_v, in_s.at[0])
    load_w = pltpu.make_async_copy(w_hbm, w_v, in_s.at[1])
    load_table.start()
    load_w.start()

    ids3[...] = jnp.full_like(ids3, -1)
    for t in range(n):
        ids3[t, :, pl.ds(0, slots)] = ids_ref[pl.ds(t, 1), :]
    hot_pad[...] = jnp.full_like(hot_pad, -1)
    hot_pad[:, pl.ds(0, hot_dev)] = hot_ids_ref[...]
    bag = bag_ref.shape[0]
    bag_rows[...] = bag_ref[...].T
    for s in range(8):
        bag2[:, pl.ds(s * bag, bag)] = bag_rows[pl.ds(s, batch // 8, stride=8), :]

    entries = 8 * bag
    tiles = vocab // 128
    own = lax.broadcasted_iota(i32, (8, entries), 1) // bag == lax.broadcasted_iota(i32, (8, entries), 0)
    tile_ids = lax.broadcasted_iota(i32, (tiles, 8, entries), 0)
    lane_ids = lax.broadcasted_iota(i32, (128, entries), 0)

    def build(i):
        outs = []
        for h in range(2):
            v = bag2[pl.ds(2 * i + h, 1), :]
            key = jnp.where(own, v >> 7, -1)
            left = (key[None] == tile_ids).astype(f32).reshape(tiles * 8, entries).astype(bf16)
            right = (lane_ids == (v & 127)).astype(f32).astype(bf16)
            outs.append(
                lax.dot_general(left, right, (((1,), (1,)), ((), ())), preferred_element_type=f32)
            )
        at = pl.ds(pl.multiple_of(16 * i, 16), 16)
        for k in range(tiles):
            t = jnp.concatenate([outs[0][8 * k : 8 * k + 8], outs[1][8 * k : 8 * k + 8]], axis=0)
            inc[at, pl.ds(k * 128, 128)] = t.astype(bf16)

    load_table.wait()
    tb[...] = table_v[...].astype(bf16)
    hot_col = to_column(eye(half, 128, c * half), hot_pad[...].astype(f32))
    hot_sel = (hot_col == lax.broadcasted_iota(i32, (half, rows), 1).astype(f32)).astype(f32).astype(bf16)
    hot[x, z, c] = jnp.dot(hot_sel, tb[...], preferred_element_type=f32).astype(bf16)
    asked[me] = ids3[me]
    over(0, pre, build)
    pl.semaphore_wait(barrier, n - 1 + NY)

    def send_ids(k):
        p = peer(k, x, z)
        remote(ids3.at[p], asked.at[me], ids_s.at[p], ids_r.at[me], dp, p).start()

    over(0, n - 1, send_ids)

    def hot_to_x(zs, xo):
        blk_ = hot.at[x, zs, c]
        remote(blk_, blk_, xb_s.at[xo, zs], xb_r.at[x, zs], dp, ((x + xo) % NX) * NZ + z).start()

    def hot_to_z(zo):
        blk_ = hot.at[x, z, c]
        remote(blk_, blk_, za_s.at[zo], za_r.at[z], dp, x * NZ + (z + zo) % NZ).start()

    over(1, NZ, hot_to_z)
    for xo in range(1, NX):
        hot_to_x(z, xo)
    over(pre, mid, build)

    def forward_x(zo):
        zs = (z + zo) % NZ
        blk_ = hot.at[x, zs, c]
        remote(blk_, blk_, za_s.at[zo], za_r.at[zs], dp, me).wait_recv()
        for xo in range(1, NX):
            hot_to_x(zs, xo)

    over(1, NZ, forward_x)
    line = hot.at[x, :, c]
    remote(line, line, cc_s.at[x], cc_r.at[x], partner, me).start()

    request = eye(slots, 128)
    chunk = served.shape[1] // slots

    def serve(ch):
        for j in range(chunk):
            k = ch * chunk + j
            p = peer(k, x, z)

            def arrived():
                remote(ids3.at[p], asked.at[p], ids_s.at[p], ids_r.at[p], dp, p).wait_recv()

            if j == chunk - 1:
                pl.when(k < n - 1)(arrived)
            else:
                arrived()
            col = to_column(request, asked[p].astype(f32))
            hit = col == lax.broadcasted_iota(i32, (slots, rows), 1).astype(f32)
            oh[pl.ds(j * slots, slots), :] = hit.astype(f32).astype(bf16)
        served[ch] = jnp.dot(oh[...], tb[...], preferred_element_type=f32).astype(bf16)
        for j in range(chunk):
            k = ch * chunk + j
            p = peer(k, x, z)
            block = served.at[ch, pl.ds(j * slots, slots)]

            def send():
                remote(block, fetched.at[me], f_s.at[p], f_r.at[me], dp, p).start()

            def keep():
                fetched[me] = served[ch, pl.ds(j * slots, slots)]

            if j == chunk - 1:
                pl.when(k < n - 1)(send)
                pl.when(k == n - 1)(keep)
            else:
                send()

    over(0, n // chunk, serve)
    over(mid, batch // 16, build)

    def line_to_partner(xo):
        xs = (x + xo) % NX

        def landed(zs):
            blk_ = hot.at[xs, zs, c]
            remote(blk_, blk_, xb_s.at[xo, zs], xb_r.at[xs, zs], dp, me).wait_recv()

        over(0, NZ, landed)
        line = hot.at[xs, :, c]
        remote(line, line, cc_s.at[xs], cc_r.at[xs], partner, me).start()

    over(1, NX, line_to_partner)

    for t in range(n):
        flat[:, pl.ds(t * slots, slots)] = asked[t][:, :slots]
    for b in range(rows // 128):
        sum_col[pl.ds(b * 128, 128), :] = to_column(eye(128, 128), sum_ref[pl.ds(b, 1), :])

    def finish_x(xs):
        line = hot.at[xs, :, 1 - c]
        remote(line, line, cc_s.at[xs], cc_r.at[xs], partner, me).wait_recv()

    over(0, NX, finish_x)
    acc[...] = jnp.dot(
        inc[:, pl.ds(0, hot_cols)], hot[...].reshape(hot_cols, width), preferred_element_type=f32
    )

    def fetched_wait(k):
        p = peer(k, x, z)
        remote(fetched.at[p], fetched.at[p], f_s.at[p], f_r.at[p], dp, p).wait_recv()

    over(0, n - 1, fetched_wait)
    slot_ids = lax.broadcasted_iota(i32, (slots, width), 0)

    def live(t):
        return slot_ids < count_ref[:, t : t + 1]

    for t in range(n):
        fetched[t] = jnp.where(live(t), fetched[t].astype(f32), 0.0).astype(bf16)
    pooled = (
        acc[...]
        + jnp.dot(
            inc[:, pl.ds(hot_cols, vocab - hot_cols)],
            fetched[...].reshape(n * slots, width),
            preferred_element_type=f32,
        )
    ).astype(bf16)

    load_w.wait()
    acc[...] = jnp.zeros_like(acc)
    hidden_units = w_v.shape[1]
    step = acc.shape[1]

    def forward(j):
        at = pl.ds(pl.multiple_of(j * step, step), step)
        pre_act = jnp.dot(pooled, w_v[:, at], preferred_element_type=f32)
        w = w_out_ref[:, at].astype(f32)
        acc[...] += jnp.maximum(pre_act, 0.0).astype(bf16).astype(f32) * w
        wm[:, at] = jnp.where(pre_act > 0, w, 0.0).astype(bf16)

    over(0, hidden_units // step, forward)
    logit = jnp.sum(acc[...], axis=1, keepdims=True)
    lab = jnp.concatenate(
        [to_column(eye(128, 128), labels_ref[:, pl.ds(b * 128, 128)]) for b in range(batch // 128)], axis=0
    )
    dlogit = jax.nn.sigmoid(logit) - lab
    dpool[...] = jnp.zeros_like(dpool)
    deep = min(1024, hidden_units)

    def backward(j):
        at = pl.ds(pl.multiple_of(j * deep, deep), deep)
        dhidden = (dlogit * wm[:, at].astype(f32)).astype(bf16)
        dpool[...] += lax.dot_general(
            dhidden, w_v[:, at], (((1,), (1,)), ((), ())), preferred_element_type=f32
        )

    over(0, hidden_units // deep, backward)
    dpooled = dpool[...].astype(bf16)

    def slot_grad(at, size):
        return lax.dot_general(
            inc[:, pl.ds(at, size)], dpooled, (((0,), (0,)), ((), ())), preferred_element_type=f32
        )

    def core_copy(q):
        at = pl.ds(q * (n // parts), n // parts)
        return remote(hot_g.at[1 - c, at], hcore.at[at], hc_s.at[q], hc_r.at[q], partner, me)

    owners = 256 // hot_dev
    for k in range(hot_cols // 256):
        g = slot_grad(k * 256, 256).reshape(owners, NY, per_y, width).astype(bf16)
        for h in range(2):
            hot_g[h, pl.ds(k * owners, owners)] = g[..., h * 128 : (h + 1) * 128]
        done = (k + 1) * parts
        if done % (hot_cols // 256) == 0:
            core_copy(done // (hot_cols // 256) - 1).start()
    cold_step = min(256, n * slots)
    for k in range(n * slots // cold_step):
        g = slot_grad(hot_cols + k * cold_step, cold_step)
        for i in range(cold_step // slots):
            t = k * (cold_step // slots) + i
            cold_g[t] = jnp.where(live(t), g[i * slots : (i + 1) * slots], 0.0).astype(bf16)

    def cold_send(k):
        p = peer(k, x, z)
        to = ret.at[pl.ds(pl.multiple_of(me * slots, slots), slots)]
        remote(cold_g.at[p], to, c_s.at[p], c_r.at[me], dp, p).start()

    def y_copy(src, yt, q):
        at = pl.ds(q * (n // parts), n // parts)
        return remote(hsum.at[yt, at], hy.at[src, at], hy_s.at[yt, q], hy_r.at[src, q], dp_of(yt), me)

    for q in range(parts):
        core_copy(q).wait_recv()
        at = pl.ds(q * (n // parts), n // parts)

        def y_send(k):
            yt = (y + k) % NY
            hsum[yt, at] = (hot_g[c, at, yt].astype(f32) + hcore[at, yt].astype(f32)).astype(bf16)

            @pl.when(k < NY)
            def _():
                y_copy(y, yt, q).start()

        over(1, NY + 1, y_send)
        if q == 0:
            over(0, n - 1, cold_send)
    ret[pl.ds(pl.multiple_of(me * slots, slots), slots), :] = cold_g[me]

    for r in range(0, rows, 128):
        ids = lax.broadcasted_iota(i32, (128, n * slots), 0) + r
        oht[pl.ds(r, 128), :] = (ids == flat[...]).astype(f32).astype(bf16)
    hfin[...] = jnp.zeros_like(hfin)

    def y_wait(k):
        ys = (y + k) % NY
        for q in range(parts):
            y_copy(ys, ys, q).wait_recv()

    over(1, NY, y_wait)
    hy[y] = hsum[y]
    tot = hy[0].astype(f32)
    for k in range(1, NY):
        tot = tot + hy[k].astype(f32)
    hz[...] = tot.astype(bf16)

    def t_send(k):
        p = peer(k, x, z)
        remote(hz.at[p], ht.at[me], ht_s.at[p], ht_r.at[me], dp, p).start()

    over(0, n - 1, t_send)
    ht[me] = hz[me]

    def cold_wait(k):
        p = peer(k, x, z)
        to = ret.at[pl.ds(pl.multiple_of(p * slots, slots), slots)]
        remote(cold_g.at[p], to, c_s.at[p], c_r.at[p], dp, p).wait_recv()

    over(0, n - 1, cold_wait)
    gacc[...] = jnp.dot(oht[...], ret[...], preferred_element_type=f32)

    def t_wait(k):
        p = peer(k, x, z)
        remote(hz.at[p], ht.at[p], ht_s.at[p], ht_r.at[p], dp, p).wait_recv()

    over(0, n - 1, t_wait)
    hot_tot = jnp.sum(ht[...].astype(f32), axis=0)
    lanes = lax.broadcasted_iota(i32, (per_y, width), 1) // 128
    hot_tot = jnp.where(lanes == c, jnp.concatenate([hot_tot, hot_tot], axis=1), 0.0)
    hfin[pl.ds(pl.multiple_of(y * per_y, 8), per_y), :] = hot_tot
    hot_rows = hfin[...].astype(bf16)

    def half_grad(cc):
        at = pl.ds(pl.multiple_of(cc * (rows // 2), 128), rows // 2)
        sel = (lax.broadcasted_iota(i32, (rows // 2, 128), 0) + cc * (rows // 2) == hot_pad[...]).astype(f32)
        g = gacc[at, :] + jnp.dot(sel.astype(bf16), hot_rows, preferred_element_type=f32)
        gl[cc] = g.astype(bf16).reshape(NY, blk, width)

    def g_core(yt):
        return remote(gl.at[1 - c, yt], gcore.at[yt], gc_s.at[yt], gc_r.at[yt], partner, me)

    def g_y(src, yt):
        return remote(gsum.at[yt], gy.at[src], gy_s.at[yt], gy_r.at[src], dp_of(yt), me)

    half_grad(1 - c)
    over(1, NY + 1, lambda k: g_core((y + k) % NY).start())
    half_grad(c)

    def g_send(k):
        yt = (y + k) % NY
        g_core(yt).wait_recv()
        gsum[yt] = (gl[c, yt].astype(f32) + gcore[yt].astype(f32)).astype(bf16)

        @pl.when(k < NY)
        def _():
            g_y(y, yt).start()

    over(1, NY + 1, g_send)
    tot = gsum[y].astype(f32)
    for k in range(1, NY):
        ys = (y + k) % NY
        g_y(ys, ys).wait_recv()
        tot = tot + gy[ys].astype(f32)
    total[c, y] = tot.astype(bf16)

    def to_y(src, yt):
        b = total.at[c, src]
        return remote(b, b, ag_s.at[yt], ag_r.at[src], dp_of(yt), me)

    def to_core(cc, yt):
        b = total.at[cc, yt]
        return remote(b, b, ac_s.at[yt], ac_r.at[yt], partner, me)

    over(1, NY, lambda k: to_y(y, (y + k) % NY).start())
    to_core(c, y).start()

    def update(cc, yy):
        at = pl.ds(pl.multiple_of((cc * NY + yy) * blk, blk), blk)
        g = total[cc, yy].astype(f32)
        new_sum = sum_col[at, :] + jnp.sum(g * g, axis=1, keepdims=True) * (1.0 / width)
        sum_col[at, :] = new_sum
        table_out[at, :] = table_v[at, :] - g * (learning_rate / jnp.sqrt(new_sum))

    update(c, y)

    def gather(k):
        ys = (y + k) % NY
        to_y(ys, ys).wait_recv()
        to_core(c, ys).start()
        update(c, ys)

    over(1, NY, gather)

    def gather_core(k):
        ys = (y + k) % NY
        to_core(1 - c, ys).wait_recv()
        update(1 - c, ys)

    over(0, NY, gather_core)
    for b in range(rows // 128):
        sum_out[pl.ds(b, 1), :] = jnp.sum(
            jnp.where(eye(128, 128), sum_col[pl.ds(b * 128, 128), :], 0.0), axis=0, keepdims=True
        )

    def finish_table(k):
        p = peer(k, x, z)
        remote(ids3.at[p], asked.at[me], ids_s.at[p], ids_r.at[me], dp, p).wait_send()
        remote(served.at[0, pl.ds(0, slots)], fetched.at[me], f_s.at[p], f_r.at[me], dp, p).wait_send()
        to = ret.at[pl.ds(pl.multiple_of(me * slots, slots), slots)]
        remote(cold_g.at[p], to, c_s.at[p], c_r.at[me], dp, p).wait_send()
        remote(hz.at[p], ht.at[me], ht_s.at[p], ht_r.at[me], dp, p).wait_send()

    over(0, n - 1, finish_table)

    def finish_hot(zo):
        blk_ = hot.at[x, z, c]

        @pl.when(zo > 0)
        def _():
            remote(blk_, blk_, za_s.at[zo], za_r.at[z], dp, me).wait_send()

        for xo in range(1, NX):
            remote(blk_, blk_, xb_s.at[xo, zo], xb_r.at[x, zo], dp, me).wait_send()

    over(0, NZ, finish_hot)

    def finish_line(xs):
        line = hot.at[xs, :, c]
        remote(line, line, cc_s.at[xs], cc_r.at[xs], partner, me).wait_send()

    over(0, NX, finish_line)
    for q in range(parts):
        core_copy(q).wait_send()

    def finish_y(k):
        yt = (y + k) % NY
        for q in range(parts):
            y_copy(y, yt, q).wait_send()
        g_y(y, yt).wait_send()
        to_y(y, yt).wait_send()

    over(1, NY, finish_y)

    def finish_core(yt):
        g_core(yt).wait_send()
        to_core(c, yt).wait_send()

    over(0, NY, finish_core)


def per_device(bag_slots, labels, cold_ids, cold_count, table, adagrad_sum, hot_ids, w_in, w_out):
    n = NX * NZ
    batch, bag = bag_slots.shape
    rows, width = table.shape
    slots = cold_ids.shape[2]
    hot_dev = hot_ids.shape[0]
    hot_cols = n * hot_dev
    vocab = n * (hot_dev + slots)
    hidden = w_in.shape[1]
    chunk = min(8, n)
    per_y = hot_dev // NY
    parts = 2 if hot_cols % 512 == 0 else 1
    blk = rows // (2 * NY)
    groups = batch // 16
    dma = pltpu.SemaphoreType.DMA
    vmem = pl.BlockSpec(memory_space=pltpu.VMEM)
    hbm = pl.BlockSpec(memory_space=pl.ANY)
    new_table, new_sum = pl.pallas_call(
        functools.partial(step_kernel, groups // 4, groups // 2),
        name="step",
        out_shape=(
            jax.ShapeDtypeStruct((rows, width), f32),
            jax.ShapeDtypeStruct((rows // 128, 128), f32),
        ),
        in_specs=[vmem, vmem, vmem, vmem, hbm, vmem, vmem, hbm, vmem],
        out_specs=(vmem, vmem),
        scratch_shapes=[
            pltpu.VMEM((rows, width), f32),
            pltpu.VMEM(w_in.shape, bf16),
            pltpu.VMEM((rows, width), bf16),
            pltpu.VMEM((n, 1, 128), i32),
            pltpu.VMEM((n, 1, 128), i32),
            pltpu.VMEM((1, n * slots), i32),
            pltpu.VMEM((1, 128), i32),
            pltpu.VMEM((batch, bag), i32),
            pltpu.VMEM((batch // 8, 8 * bag), i32),
            pltpu.VMEM((rows, 1), f32),
            pltpu.VMEM((NX, NZ, 2, hot_dev // 2, width), bf16),
            pltpu.VMEM((n, slots, width), bf16),
            pltpu.VMEM((chunk * slots, rows), bf16),
            pltpu.VMEM((n // chunk, chunk * slots, width), bf16),
            pltpu.VMEM((batch, vocab), bf16),
            pltpu.VMEM((batch, hidden), bf16),
            pltpu.VMEM((batch, 256), f32),
            pltpu.VMEM((batch, width), f32),
            pltpu.VMEM((2, n, NY, per_y, 128), bf16),
            pltpu.VMEM((n, slots, width), bf16),
            pltpu.VMEM((n, NY, per_y, 128), bf16),
            pltpu.VMEM((NY, n, per_y, 128), bf16),
            pltpu.VMEM((NY, n, per_y, 128), bf16),
            pltpu.VMEM((n, per_y, 128), bf16),
            pltpu.VMEM((n, per_y, 128), bf16),
            pltpu.VMEM((n * slots, width), bf16),
            pltpu.VMEM((rows, n * slots), bf16),
            pltpu.VMEM((rows, width), f32),
            pltpu.VMEM((128, width), f32),
            pltpu.VMEM((2, NY, blk, width), bf16),
            pltpu.VMEM((NY, blk, width), bf16),
            pltpu.VMEM((NY, blk, width), bf16),
            pltpu.VMEM((NY, blk, width), bf16),
            pltpu.VMEM((2, NY, blk, width), bf16),
            dma((2,)),
            dma((n,)), dma((n,)),
            dma((NZ,)), dma((NZ,)),
            dma((NX, NZ)), dma((NX, NZ)),
            dma((NX,)), dma((NX,)),
            dma((n,)), dma((n,)),
            dma((parts,)), dma((parts,)),
            dma((NY, parts)), dma((NY, parts)),
            dma((n,)), dma((n,)),
            dma((n,)), dma((n,)),
            dma((NY,)), dma((NY,)),
            dma((NY,)), dma((NY,)),
            dma((NY,)), dma((NY,)),
            dma((NY,)), dma((NY,)),
        ],
        compiler_params=pltpu.CompilerParams(
            collective_id=0, has_side_effects=True, vmem_limit_bytes=60 << 20
        ),
    )(
        bag_slots.T,
        labels.reshape(1, batch),
        cold_ids[0],
        cold_count,
        table,
        adagrad_sum.reshape(rows // 128, 128),
        hot_ids.reshape(1, hot_dev),
        w_in,
        w_out.reshape(1, hidden),
    )
    return new_table, new_sum.reshape(rows)


def solution(mesh):
    placed = (
        P(("dp", "table"), None),
        P(("dp", "table")),
        P(("dp", "table"), None, None),
        P(("dp", "table"), None),
        P("table", None),
        P("table"),
        P("table"),
        P(),
        P(),
    )
    return jax.shard_map(
        per_device,
        mesh=mesh,
        in_specs=placed,
        out_specs=(P("table", None), P("table")),
        check_vma=False,
    )
```

time: 547 us -> 101 us (0.18)
  waiting for transfers between devices: 327 us -> 0 us
  other arithmetic: 136 us -> 0 us
  Pallas kernels: 0 us -> 95.9 us
  blocking collectives: 22.3 us -> 0 us
  matrix products: 19.2 us -> 0 us
  starting transfers between devices: 13.5 us -> 0 us
  between operations: 14 us -> 0.65 us
  local copies, waits for them, and re-layouts: 14.6 us -> 4.17 us
    reduce_scatter x1 -> x0, waiting for transfers between devices: 208 us -> none  [per_device(): lax.psum_scatter(lax.dot_general(columns, dpooled, (((0,), (0,)), ((), ()...]
    psum x1 -> x0, waiting for transfers between devices: 119 us -> none  [per_device(): total_grad = lax.psum(grad.astype(jnp.bfloat16), 'dp').astype(jnp.float32)]
    unnamed x4 -> x0, other arithmetic: 115 us -> none
    pallas_call x0 -> x1, Pallas kernels: none -> 95.9 us  [per_device(): pl.pallas_call(functools.partial(step_kernel, groups // 4, groups // 2),...]
    all_to_all x1 -> x0, blocking collectives: 22.3 us -> none  [per_device(): lax.all_to_all(cold_ids[0], 'table', split_axis=0, concat_axis=0, tiled=T...]
    dot_general x6 -> x0, matrix products: 19.2 us -> none  [the longest x1 7.93 us: per_device(): pre_act = jnp.dot(pooled, w_in, preferred_element_type=jnp.float32)]
    all_to_all x2 -> x0, starting transfers between devices: 13.4 us -> none  [the longest x1 9.49 us: per_device(): lax.all_to_all(cold_term.astype(jnp.bfloat16), 'table', split_axis=0, con...]
    scatter-add x2 -> x0, other arithmetic: 10.8 us -> none  [the longest x1 8.65 us: per_device(): grad = grad.at[asked_ids.reshape(-1)].add(returned.reshape(-1, width))]
  transfers between devices with their start and end apart: 5 -> 0, of which waited for: 2 -> 0; matrix products, arithmetic and copies ran while one was open for 25% -> 0% of each run, Pallas kernels for 0% -> 0%
where the time goes in v2:
time: 101 us
  Pallas kernels  95.9 us (95%)
  local copies, waits for them, and re-layouts  4.17 us (4%)
    pallas_call x1, Pallas kernels, per_device(): pl.pallas_call(functools.partial(step_kernel, groups // 4, groups // 2),...  95.9 us
    unnamed x4, local copies, waits for them, and re-layouts  2.86 us

profile of v2, /device:TPU:1, one launch (start us, length us, event | category | flops | bytes accessed | tf_op | source)
XLA Modules:
  0.0 100.7 jit_solution(8787114110124542412)
XLA Ops:
  0.6 1.3 %reshape.22.w_out_ref = bf16[1,4096]{1,0:T(2,128)(2,1)} reshape(bf16[4096]{0:T(1024)(128)(2,1)} %param.17) | data formatting | bytes 16384 | tf_op jit(solution)/shard_map/reshape | solution.py:579
  1.9 95.9 %step.1 = (f32[1024,256]{1,0:T(8,128)}, f32[8,128]{1,0:T(8,128)}) custom-call(s32[32,512]{1,0:T(8,128)} %bitcast.6, f32[1,512]{1,0:T(1,128)} %bitcast.10, s32[32,32]{1,0:T(8,128)} %bitcast.7, s32[1,32]{1,0:T(1,128)} %count_ref.1, f32[1024,256]{1,0:T(8,128)} %table_hbm.1, f32[8,128]{1,0:T(8,128)} %bitcast.8, s32[1,64]{1,0:T(1,128)} %bitcast.11, ...), custom_call_target="tpu_custom_call" | custom-call | tf_op jit(solution)/shard_map/step/pallas_call | solution.py:508
  97.9 0.0 copy-start
  97.9 2.3 %copy.13 = f32[1024,256]{1,0:T(8,128)} copy(f32[1024,256]{1,0:T(8,128)} %get-tuple-element.8) | data formatting | bytes 2097152
  100.1 0.0 copy-done
  100.2 0.6 copy.14
Async XLA Ops:
  97.9 2.3 %copy-start = (f32[8,128]{1,0:T(8,128)S(1)}, f32[8,128]{1,0:T(8,128)}, u32[]{:S(2)}) copy-start(f32[8,128]{1,0:T(8,128)} %get-tuple-element.5) | copy-start | bytes 12292

commit v3 on v2

--- a/solution.py
+++ b/solution.py
@@ -45,9 +45,9 @@
     table_out, sum_out,
     table_v, w_v, tb, ids3, asked, flat, hot_pad, bag_rows, bag2, sum_col,
     hot, fetched, oh, served, inc, wm, acc, dpool,
-    hot_g, cold_g, hcore, hsum, hy, hz, ht, ret, oht, gacc, hfin, gl, gcore, gsum, gy, total,
+    hot_g, cold_g, hcore, hsum, hy, hz, ht, ret, oht, gacc, hfin, hsel, hotf, w_row, gl, gcore, gsum, gy, total,
     in_s, ids_s, ids_r, za_s, za_r, xb_s, xb_r, cc_s, cc_r, f_s, f_r,
-    hc_s, hc_r, hy_s, hy_r, ht_s, ht_r, c_s, c_r, gc_s, gc_r, gy_s, gy_r, ag_s, ag_r, ac_s, ac_r,
+    hc_s, hc_r, hy_s, hy_r, ht_s, ht_r, c_s, c_r, gc_s, gc_r, gy_s, gy_r, ag_s, ag_r, ac_s, ac_r, ha_s, ha_r,
 ):
     n = NX * NZ
     dp, me, y, c, x, z, partner = place()
@@ -64,12 +64,12 @@
     def dp_of(yy):
         return yy * 2 + c
 
-    def over(lo, hi, body):
+    def over(lo, hi, body, unroll=1):
         def run(k, _):
             body(k)
             return 0
 
-        lax.fori_loop(lo, hi, run, 0)
+        lax.fori_loop(lo, hi, run, 0, unroll=unroll)
 
     def eye(a, b, shift=0):
         return lax.broadcasted_iota(i32, (a, b), 0) + shift == lax.broadcasted_iota(i32, (a, b), 1)
@@ -80,9 +80,8 @@
     barrier = pltpu.get_barrier_semaphore()
     over(0, n - 1, lambda k: pl.semaphore_signal(
         barrier, inc=1, device_id=(dp, peer(k, x, z)), device_id_type=MESH))
-    over(1, NY, lambda k: pl.semaphore_signal(
-        barrier, inc=1, device_id=(dp_of((y + k) % NY), me), device_id_type=MESH))
-    pl.semaphore_signal(barrier, inc=1, device_id=(partner, me), device_id_type=MESH)
+    over(1, 2 * NY, lambda k: pl.semaphore_signal(
+        barrier, inc=1, device_id=((dp + k) % (2 * NY), me), device_id_type=MESH))
 
     load_table = pltpu.make_async_copy(table_hbm, table_v, in_s.at[0])
     load_w = pltpu.make_async_copy(w_hbm, w_v, in_s.at[1])
@@ -94,6 +93,8 @@
         ids3[t, :, pl.ds(0, slots)] = ids_ref[pl.ds(t, 1), :]
     hot_pad[...] = jnp.full_like(hot_pad, -1)
     hot_pad[:, pl.ds(0, hot_dev)] = hot_ids_ref[...]
+    for k in range(w_out_ref.shape[0]):
+        w_row[:, pl.ds(k * 128, 128)] = w_out_ref[pl.ds(k, 1), :].astype(f32)
     bag = bag_ref.shape[0]
     bag_rows[...] = bag_ref[...].T
     for s in range(8):
@@ -127,7 +128,7 @@
     hot[x, z, c] = jnp.dot(hot_sel, tb[...], preferred_element_type=f32).astype(bf16)
     asked[me] = ids3[me]
     over(0, pre, build)
-    pl.semaphore_wait(barrier, n - 1 + NY)
+    pl.semaphore_wait(barrier, n - 1 + 2 * NY - 1)
 
     def send_ids(k):
         p = peer(k, x, z)
@@ -165,7 +166,7 @@
     def serve(ch):
         for j in range(chunk):
             k = ch * chunk + j
-            p = peer(k, x, z)
+            p = peer((2 * n - 2 - k) % n, x, z)
 
             def arrived():
                 remote(ids3.at[p], asked.at[p], ids_s.at[p], ids_r.at[p], dp, p).wait_recv()
@@ -180,7 +181,7 @@
         served[ch] = jnp.dot(oh[...], tb[...], preferred_element_type=f32).astype(bf16)
         for j in range(chunk):
             k = ch * chunk + j
-            p = peer(k, x, z)
+            p = peer((2 * n - 2 - k) % n, x, z)
             block = served.at[ch, pl.ds(j * slots, slots)]
 
             def send():
@@ -254,11 +255,11 @@
     def forward(j):
         at = pl.ds(pl.multiple_of(j * step, step), step)
         pre_act = jnp.dot(pooled, w_v[:, at], preferred_element_type=f32)
-        w = w_out_ref[:, at].astype(f32)
+        w = w_row[:, at]
         acc[...] += jnp.maximum(pre_act, 0.0).astype(bf16).astype(f32) * w
         wm[:, at] = jnp.where(pre_act > 0, w, 0.0).astype(bf16)
 
-    over(0, hidden_units // step, forward)
+    over(0, hidden_units // step, forward, unroll=2)
     logit = jnp.sum(acc[...], axis=1, keepdims=True)
     lab = jnp.concatenate(
         [to_column(eye(128, 128), labels_ref[:, pl.ds(b * 128, 128)]) for b in range(batch // 128)], axis=0
@@ -286,6 +287,19 @@
         at = pl.ds(q * (n // parts), n // parts)
         return remote(hot_g.at[1 - c, at], hcore.at[at], hc_s.at[q], hc_r.at[q], partner, me)
 
+    cold_step = min(256, n * slots)
+    for k in range(n * slots // cold_step):
+        g = slot_grad(hot_cols + k * cold_step, cold_step)
+        for i in range(cold_step // slots):
+            t = k * (cold_step // slots) + i
+            cold_g[t] = jnp.where(live(t), g[i * slots : (i + 1) * slots], 0.0).astype(bf16)
+
+    def cold_send(k):
+        p = peer(k, x, z)
+        to = ret.at[pl.ds(pl.multiple_of(me * slots, slots), slots)]
+        remote(cold_g.at[p], to, c_s.at[p], c_r.at[me], dp, p).start()
+
+    over(0, n - 1, cold_send)
     owners = 256 // hot_dev
     for k in range(hot_cols // 256):
         g = slot_grad(k * 256, 256).reshape(owners, NY, per_y, width).astype(bf16)
@@ -294,22 +308,14 @@
         done = (k + 1) * parts
         if done % (hot_cols // 256) == 0:
             core_copy(done // (hot_cols // 256) - 1).start()
-    cold_step = min(256, n * slots)
-    for k in range(n * slots // cold_step):
-        g = slot_grad(hot_cols + k * cold_step, cold_step)
-        for i in range(cold_step // slots):
-            t = k * (cold_step // slots) + i
-            cold_g[t] = jnp.where(live(t), g[i * slots : (i + 1) * slots], 0.0).astype(bf16)
-
-    def cold_send(k):
-        p = peer(k, x, z)
-        to = ret.at[pl.ds(pl.multiple_of(me * slots, slots), slots)]
-        remote(cold_g.at[p], to, c_s.at[p], c_r.at[me], dp, p).start()
 
     def y_copy(src, yt, q):
         at = pl.ds(q * (n // parts), n // parts)
         return remote(hsum.at[yt, at], hy.at[src, at], hy_s.at[yt, q], hy_r.at[src, q], dp_of(yt), me)
 
+    for r in range(0, rows, 128):
+        ids = lax.broadcasted_iota(i32, (128, n * slots), 0) + r
+        oht[pl.ds(r, 128), :] = (ids == flat[...]).astype(f32).astype(bf16)
     for q in range(parts):
         core_copy(q).wait_recv()
         at = pl.ds(q * (n // parts), n // parts)
@@ -323,14 +329,42 @@
                 y_copy(y, yt, q).start()
 
         over(1, NY + 1, y_send)
-        if q == 0:
-            over(0, n - 1, cold_send)
     ret[pl.ds(pl.multiple_of(me * slots, slots), slots), :] = cold_g[me]
-
-    for r in range(0, rows, 128):
-        ids = lax.broadcasted_iota(i32, (128, n * slots), 0) + r
-        oht[pl.ds(r, 128), :] = (ids == flat[...]).astype(f32).astype(bf16)
+    hsel[...] = (lax.broadcasted_iota(i32, (rows, 128), 0) == hot_pad[...]).astype(f32).astype(bf16)
     hfin[...] = jnp.zeros_like(hfin)
+
+    def cold_wait(k):
+        p = peer(k, x, z)
+        to = ret.at[pl.ds(pl.multiple_of(p * slots, slots), slots)]
+        remote(cold_g.at[p], to, c_s.at[p], c_r.at[p], dp, p).wait_recv()
+
+    over(0, n - 1, cold_wait)
+
+    def half_grad(cc):
+        at = pl.ds(pl.multiple_of(cc * (rows // 2), 128), rows // 2)
+        g = jnp.dot(oht[at, :], ret[...], preferred_element_type=f32)
+        gl[cc] = g.astype(bf16).reshape(NY, blk, width)
+
+    def g_core(yt):
+        return remote(gl.at[1 - c, yt], gcore.at[yt], gc_s.at[yt], gc_r.at[yt], partner, me)
+
+    def g_y(src, yt):
+        return remote(gsum.at[yt], gy.at[src], gy_s.at[yt], gy_r.at[src], dp_of(yt), me)
+
+    half_grad(1 - c)
+    over(1, NY + 1, lambda k: g_core((y + k) % NY).start())
+    half_grad(c)
+
+    def g_send(k):
+        yt = (y + k) % NY
+        g_core(yt).wait_recv()
+        gsum[yt] = (gl[c, yt].astype(f32) + gcore[yt].astype(f32)).astype(bf16)
+
+        @pl.when(k < NY)
+        def _():
+            g_y(y, yt).start()
+
+    over(1, NY + 1, g_send)
 
     def y_wait(k):
         ys = (y + k) % NY
@@ -351,51 +385,6 @@
     over(0, n - 1, t_send)
     ht[me] = hz[me]
 
-    def cold_wait(k):
-        p = peer(k, x, z)
-        to = ret.at[pl.ds(pl.multiple_of(p * slots, slots), slots)]
-        remote(cold_g.at[p], to, c_s.at[p], c_r.at[p], dp, p).wait_recv()
-
-    over(0, n - 1, cold_wait)
-    gacc[...] = jnp.dot(oht[...], ret[...], preferred_element_type=f32)
-
-    def t_wait(k):
-        p = peer(k, x, z)
-        remote(hz.at[p], ht.at[p], ht_s.at[p], ht_r.at[p], dp, p).wait_recv()
-
-    over(0, n - 1, t_wait)
-    hot_tot = jnp.sum(ht[...].astype(f32), axis=0)
-    lanes = lax.broadcasted_iota(i32, (per_y, width), 1) // 128
-    hot_tot = jnp.where(lanes == c, jnp.concatenate([hot_tot, hot_tot], axis=1), 0.0)
-    hfin[pl.ds(pl.multiple_of(y * per_y, 8), per_y), :] = hot_tot
-    hot_rows = hfin[...].astype(bf16)
-
-    def half_grad(cc):
-        at = pl.ds(pl.multiple_of(cc * (rows // 2), 128), rows // 2)
-        sel = (lax.broadcasted_iota(i32, (rows // 2, 128), 0) + cc * (rows // 2) == hot_pad[...]).astype(f32)
-        g = gacc[at, :] + jnp.dot(sel.astype(bf16), hot_rows, preferred_element_type=f32)
-        gl[cc] = g.astype(bf16).reshape(NY, blk, width)
-
-    def g_core(yt):
-        return remote(gl.at[1 - c, yt], gcore.at[yt], gc_s.at[yt], gc_r.at[yt], partner, me)
-
-    def g_y(src, yt):
-        return remote(gsum.at[yt], gy.at[src], gy_s.at[yt], gy_r.at[src], dp_of(yt), me)
-
-    half_grad(1 - c)
-    over(1, NY + 1, lambda k: g_core((y + k) % NY).start())
-    half_grad(c)
-
-    def g_send(k):
-        yt = (y + k) % NY
-        g_core(yt).wait_recv()
-        gsum[yt] = (gl[c, yt].astype(f32) + gcore[yt].astype(f32)).astype(bf16)
-
-        @pl.when(k < NY)
-        def _():
-            g_y(y, yt).start()
-
-    over(1, NY + 1, g_send)
     tot = gsum[y].astype(f32)
     for k in range(1, NY):
         ys = (y + k) % NY
@@ -414,9 +403,31 @@
     over(1, NY, lambda k: to_y(y, (y + k) % NY).start())
     to_core(c, y).start()
 
+    def t_wait(k):
+        p = peer(k, x, z)
+        remote(hz.at[p], ht.at[p], ht_s.at[p], ht_r.at[p], dp, p).wait_recv()
+
+    over(0, n - 1, t_wait)
+    hotf[c, pl.ds(pl.multiple_of(y * per_y, 8), per_y), :] = jnp.sum(ht[...].astype(f32), axis=0)
+
+    def h_copy(src, to):
+        b = hotf.at[src % 2, pl.ds(pl.multiple_of(src // 2 * per_y, 8), per_y)]
+        return remote(b, b, ha_s.at[to], ha_r.at[src], to, me)
+
+    over(1, 2 * NY, lambda k: h_copy(dp, (dp + k) % (2 * NY)).start())
+
+    def h_wait(k):
+        src = (dp + k) % (2 * NY)
+        h_copy(src, src).wait_recv()
+
+    over(1, 2 * NY, h_wait)
+    for h in range(2):
+        hfin[pl.ds(0, hot_dev), pl.ds(h * 128, 128)] = hotf[h]
+    gacc[...] = jnp.dot(hsel[...], hfin[...].astype(bf16), preferred_element_type=f32)
+
     def update(cc, yy):
         at = pl.ds(pl.multiple_of((cc * NY + yy) * blk, blk), blk)
-        g = total[cc, yy].astype(f32)
+        g = total[cc, yy].astype(f32) + gacc[at, :]
         new_sum = sum_col[at, :] + jnp.sum(g * g, axis=1, keepdims=True) * (1.0 / width)
         sum_col[at, :] = new_sum
         table_out[at, :] = table_v[at, :] - g * (learning_rate / jnp.sqrt(new_sum))
@@ -480,12 +491,24 @@
         to_y(y, yt).wait_send()
 
     over(1, NY, finish_y)
+    over(1, 2 * NY, lambda k: h_copy(dp, (dp + k) % (2 * NY)).wait_send())
 
     def finish_core(yt):
         g_core(yt).wait_send()
         to_core(c, yt).wait_send()
 
     over(0, NY, finish_core)
+
+
+def emit_kernel(table_ref, sum_ref, table_out, sum_out, sems):
+    copies = [
+        pltpu.make_async_copy(table_ref, table_out, sems.at[0]),
+        pltpu.make_async_copy(sum_ref, sum_out, sems.at[1]),
+    ]
+    for copy in copies:
+        copy.start()
+    for copy in copies:
+        copy.wait()
 
 
 def per_device(bag_slots, labels, cold_ids, cold_count, table, adagrad_sum, hot_ids, w_in, w_out):
@@ -544,6 +567,9 @@
             pltpu.VMEM((rows, n * slots), bf16),
             pltpu.VMEM((rows, width), f32),
             pltpu.VMEM((128, width), f32),
+            pltpu.VMEM((rows, 128), bf16),
+            pltpu.VMEM((2, hot_dev, 128), f32),
+            pltpu.VMEM((1, hidden), f32),
             pltpu.VMEM((2, NY, blk, width), bf16),
             pltpu.VMEM((NY, blk, width), bf16),
             pltpu.VMEM((NY, blk, width), bf16),
@@ -563,6 +589,7 @@
             dma((NY,)), dma((NY,)),
             dma((NY,)), dma((NY,)),
             dma((NY,)), dma((NY,)),
+            dma((2 * NY,)), dma((2 * NY,)),
         ],
         compiler_params=pltpu.CompilerParams(
             collective_id=0, has_side_effects=True, vmem_limit_bytes=60 << 20
@@ -576,9 +603,20 @@
         adagrad_sum.reshape(rows // 128, 128),
         hot_ids.reshape(1, hot_dev),
         w_in,
-        w_out.reshape(1, hidden),
+        w_out.reshape(hidden // 128, 128),
     )
-    return new_table, new_sum.reshape(rows)
+    out_table, out_sum = pl.pallas_call(
+        emit_kernel,
+        name="emit",
+        out_shape=(
+            jax.ShapeDtypeStruct((rows, width), f32),
+            jax.ShapeDtypeStruct((rows // 128, 128), f32),
+        ),
+        in_specs=[vmem, vmem],
+        out_specs=(hbm, hbm),
+        scratch_shapes=[dma((2,))],
+    )(new_table, new_sum)
+    return out_table, out_sum.reshape(rows)
 
 
 def solution(mesh):

time: 101 us -> 95.1 us (0.942)
  local copies, waits for them, and re-layouts: 4.17 us -> 0 us
  Pallas kernels: 95.9 us -> 94.3 us
    pallas_call x1, Pallas kernels: 95.9 us -> 92.1 us  [per_device(): pl.pallas_call(functools.partial(step_kernel, groups // 4, groups // 2),...]
    unnamed x4 -> x0, local copies, waits for them, and re-layouts: 2.86 us -> none
    pallas_call x0 -> x1, Pallas kernels: none -> 2.22 us  [per_device(): pl.pallas_call(emit_kernel, name='emit', out_shape=(jax.ShapeDtypeStruct(...]
    reshape x1 -> x0, local copies, waits for them, and re-layouts: 1.31 us -> none  [per_device(): w_out.reshape(1, hidden)]
where the time goes in v3:
time: 95.1 us; the launch traced here: 94.9 us
  Pallas kernels  94.3 us (99%)
    pallas_call x1, Pallas kernels, per_device(): pl.pallas_call(functools.partial(step_kernel, groups // 4, groups // 2),...  92.1 us
    pallas_call x1, Pallas kernels, per_device(): pl.pallas_call(emit_kernel, name='emit', out_shape=(jax.ShapeDtypeStruct(...  2.22 us

profile of v3, /device:TPU:1, one launch (start us, length us, event | category | flops | bytes accessed | tf_op | source)
XLA Modules:
  0.0 94.9 jit_solution(2709629503649187827)
XLA Ops:
  0.6 92.1 %step.1 = (f32[1024,256]{1,0:T(8,128)}, f32[8,128]{1,0:T(8,128)}) custom-call(s32[32,512]{1,0:T(8,128)} %bitcast.7, f32[1,512]{1,0:T(1,128)} %bitcast.11, s32[32,32]{1,0:T(8,128)} %bitcast.8, s32[1,32]{1,0:T(1,128)} %count_ref.1, f32[1024,256]{1,0:T(8,128)} %table_hbm.1, f32[8,128]{1,0:T(8,128)} %bitcast.10, s32[1,64]{1,0:T(1,128)} %bitcast.12, ...), custom_call_target="tpu_custom_call" | custom-call | tf_op jit(solution)/shard_map/step/pallas_call | solution.py:531
  92.7 2.2 %emit.1 = (f32[1024,256]{1,0:T(8,128)}, f32[8,128]{1,0:T(8,128)}) custom-call(f32[1024,256]{1,0:T(8,128)} %get-tuple-element.6.table_ref, f32[8,128]{1,0:T(8,128)} %get-tuple-element.7.sum_ref), custom_call_target="tpu_custom_call" | custom-call | tf_op jit(solution)/shard_map/emit/pallas_call | solution.py:608

commit v4 on v3

--- a/solution.py
+++ b/solution.py
@@ -31,6 +31,10 @@
     return ((x + kx) % NX) * NZ + (z + kz) % NZ
 
 
+def y_peer(k, y):
+    return (y + NY // 2 + (1 - 2 * (k % 2)) * ((k + 1) // 2)) % NY
+
+
 def place():
     dp, me = lax.axis_index("dp"), lax.axis_index("table")
     y, c = dp // 2, dp % 2
@@ -41,12 +45,13 @@
 
 def step_kernel(
     pre, mid,
-    bag_ref, labels_ref, ids_ref, count_ref, table_hbm, sum_ref, hot_ids_ref, w_hbm, w_out_ref,
+    table_hbm, w_hbm, bag_hbm, labels_hbm, ids_hbm, count_hbm, sum_hbm, hot_ids_hbm, w_out_hbm,
     table_out, sum_out,
+    bag_ref, labels_ref, ids_ref, count_ref, sum_ref, hot_ids_ref, w_out_ref,
     table_v, w_v, tb, ids3, asked, flat, hot_pad, bag_rows, bag2, sum_col,
     hot, fetched, oh, served, inc, wm, acc, dpool,
-    hot_g, cold_g, hcore, hsum, hy, hz, ht, ret, oht, gacc, hfin, hsel, hotf, w_row, gl, gcore, gsum, gy, total,
-    in_s, ids_s, ids_r, za_s, za_r, xb_s, xb_r, cc_s, cc_r, f_s, f_r,
+    hot_g, cold_g, hcore, hsum, hy, hz, ht, ret, oht, gacc, hfin, hsel, hotf, w_row, gl, gcore, gsum, gy, total, new_rows,
+    in_s, out_s, ids_s, ids_r, za_s, za_r, xb_s, xb_r, cc_s, cc_r, f_s, f_r,
     hc_s, hc_r, hy_s, hy_r, ht_s, ht_r, c_s, c_r, gc_s, gc_r, gy_s, gy_r, ag_s, ag_r, ac_s, ac_r, ha_s, ha_r,
 ):
     n = NX * NZ
@@ -59,7 +64,7 @@
     per_y = hz.shape[1]
     batch, vocab = inc.shape
     parts = hc_s.shape[0]
-    blk = gl.shape[2]
+    subs, sub = gl.shape[1], gl.shape[3]
 
     def dp_of(yy):
         return yy * 2 + c
@@ -83,10 +88,21 @@
     over(1, 2 * NY, lambda k: pl.semaphore_signal(
         barrier, inc=1, device_id=((dp + k) % (2 * NY), me), device_id_type=MESH))
 
+    small = (
+        (ids_hbm, ids_ref), (hot_ids_hbm, hot_ids_ref), (bag_hbm, bag_ref), (w_out_hbm, w_out_ref),
+        (count_hbm, count_ref), (sum_hbm, sum_ref), (labels_hbm, labels_ref),
+    )
+    loads = [pltpu.make_async_copy(a, b, in_s.at[i + 2]) for i, (a, b) in enumerate(small)]
     load_table = pltpu.make_async_copy(table_hbm, table_v, in_s.at[0])
     load_w = pltpu.make_async_copy(w_hbm, w_v, in_s.at[1])
+    for load in loads[:2]:
+        load.start()
     load_table.start()
+    for load in loads[2:]:
+        load.start()
     load_w.start()
+    for load in loads:
+        load.wait()
 
     ids3[...] = jnp.full_like(ids3, -1)
     for t in range(n):
@@ -259,7 +275,7 @@
         acc[...] += jnp.maximum(pre_act, 0.0).astype(bf16).astype(f32) * w
         wm[:, at] = jnp.where(pre_act > 0, w, 0.0).astype(bf16)
 
-    over(0, hidden_units // step, forward, unroll=2)
+    over(0, hidden_units // step, forward, unroll=4)
     logit = jnp.sum(acc[...], axis=1, keepdims=True)
     lab = jnp.concatenate(
         [to_column(eye(128, 128), labels_ref[:, pl.ds(b * 128, 128)]) for b in range(batch // 128)], axis=0
@@ -321,14 +337,14 @@
         at = pl.ds(q * (n // parts), n // parts)
 
         def y_send(k):
-            yt = (y + k) % NY
+            yt = y_peer(k, y)
             hsum[yt, at] = (hot_g[c, at, yt].astype(f32) + hcore[at, yt].astype(f32)).astype(bf16)
 
-            @pl.when(k < NY)
+            @pl.when(k < NY - 1)
             def _():
                 y_copy(y, yt, q).start()
 
-        over(1, NY + 1, y_send)
+        over(0, NY, y_send)
     ret[pl.ds(pl.multiple_of(me * slots, slots), slots), :] = cold_g[me]
     hsel[...] = (lax.broadcasted_iota(i32, (rows, 128), 0) == hot_pad[...]).astype(f32).astype(bf16)
     hfin[...] = jnp.zeros_like(hfin)
@@ -340,31 +356,37 @@
 
     over(0, n - 1, cold_wait)
 
-    def half_grad(cc):
-        at = pl.ds(pl.multiple_of(cc * (rows // 2), 128), rows // 2)
+    pieces = 2
+    per = subs // pieces
+    piece_rows = rows // 2 // pieces
+
+    def piece_grad(cc, i):
+        at = pl.ds(pl.multiple_of(cc * (rows // 2) + i * piece_rows, piece_rows), piece_rows)
         g = jnp.dot(oht[at, :], ret[...], preferred_element_type=f32)
-        gl[cc] = g.astype(bf16).reshape(NY, blk, width)
-
-    def g_core(yt):
-        return remote(gl.at[1 - c, yt], gcore.at[yt], gc_s.at[yt], gc_r.at[yt], partner, me)
-
-    def g_y(src, yt):
-        return remote(gsum.at[yt], gy.at[src], gy_s.at[yt], gy_r.at[src], dp_of(yt), me)
-
-    half_grad(1 - c)
-    over(1, NY + 1, lambda k: g_core((y + k) % NY).start())
-    half_grad(c)
+        gl[cc, pl.ds(i * per, per)] = g.astype(bf16).reshape(per, NY, sub, width)
+
+    def g_core(b, yt):
+        return remote(gl.at[1 - c, b, yt], gcore.at[b, yt], gc_s.at[b, yt], gc_r.at[b, yt], partner, me)
+
+    def g_y(b, src, yt):
+        return remote(gsum.at[b, yt], gy.at[b, src], gy_s.at[b, yt], gy_r.at[b, src], dp_of(yt), me)
+
+    for i in range(pieces):
+        piece_grad(1 - c, i)
+        over(0, per * NY, lambda k: g_core(i * per + k // NY, y_peer(k % NY, y)).start())
 
     def g_send(k):
-        yt = (y + k) % NY
-        g_core(yt).wait_recv()
-        gsum[yt] = (gl[c, yt].astype(f32) + gcore[yt].astype(f32)).astype(bf16)
-
-        @pl.when(k < NY)
+        b, yt = k // NY, y_peer(k % NY, y)
+        g_core(b, yt).wait_recv()
+        gsum[b, yt] = (gl[c, b, yt].astype(f32) + gcore[b, yt].astype(f32)).astype(bf16)
+
+        @pl.when(k % NY < NY - 1)
         def _():
-            g_y(y, yt).start()
-
-    over(1, NY + 1, g_send)
+            g_y(b, y, yt).start()
+
+    for i in range(pieces):
+        piece_grad(c, i)
+        over(i * per * NY, (i + 1) * per * NY, g_send)
 
     def y_wait(k):
         ys = (y + k) % NY
@@ -385,23 +407,25 @@
     over(0, n - 1, t_send)
     ht[me] = hz[me]
 
-    tot = gsum[y].astype(f32)
-    for k in range(1, NY):
-        ys = (y + k) % NY
-        g_y(ys, ys).wait_recv()
-        tot = tot + gy[ys].astype(f32)
-    total[c, y] = tot.astype(bf16)
-
-    def to_y(src, yt):
-        b = total.at[c, src]
-        return remote(b, b, ag_s.at[yt], ag_r.at[src], dp_of(yt), me)
-
-    def to_core(cc, yt):
-        b = total.at[cc, yt]
-        return remote(b, b, ac_s.at[yt], ac_r.at[yt], partner, me)
-
-    over(1, NY, lambda k: to_y(y, (y + k) % NY).start())
-    to_core(c, y).start()
+    def to_y(b, src, yt):
+        part = total.at[c, b, src]
+        return remote(part, part, ag_s.at[b, yt], ag_r.at[b, src], dp_of(yt), me)
+
+    def to_core(cc, b, yt):
+        part = total.at[cc, b, yt]
+        return remote(part, part, ac_s.at[b, yt], ac_r.at[b, yt], partner, me)
+
+    def dp_sum(b):
+        over(1, NY, lambda k: g_y(b, (y + k) % NY, (y + k) % NY).wait_recv())
+        gy[b, y] = gsum[b, y]
+        tot = gy[b, 0].astype(f32)
+        for k in range(1, NY):
+            tot = tot + gy[b, k].astype(f32)
+        total[c, b, y] = tot.astype(bf16)
+        over(0, NY - 1, lambda k: to_y(b, y, y_peer(k, y)).start())
+        to_core(c, b, y).start()
+
+    over(0, subs, dp_sum)
 
     def t_wait(k):
         p = peer(k, x, z)
@@ -420,38 +444,52 @@
         src = (dp + k) % (2 * NY)
         h_copy(src, src).wait_recv()
 
+    def leave(cc, b):
+        at = pl.ds(pl.multiple_of((cc * subs + b) * NY * sub, NY * sub), NY * sub)
+        return pltpu.make_async_copy(new_rows.at[at], table_out.at[at], out_s.at[cc, b])
+
+    def update(cc, b):
+        tall = NY * sub
+        at = pl.ds(pl.multiple_of((cc * subs + b) * tall, tall), tall)
+        g = total[cc, b].astype(f32).reshape(tall, width) + gacc[at, :]
+        new_sum = sum_col[at, :] + jnp.sum(g * g, axis=1, keepdims=True) * (1.0 / width)
+        sum_col[at, :] = new_sum
+        new_rows[at, :] = table_v[at, :] - g * (learning_rate / jnp.sqrt(new_sum))
+        leave(cc, b).start()
+
+    def gather(b):
+        def landed(k):
+            ys = (y + k) % NY
+            to_y(b, ys, ys).wait_recv()
+            to_core(c, b, ys).start()
+
+        over(1, NY, landed)
+
+    over(0, subs // 2, gather)
     over(1, 2 * NY, h_wait)
     for h in range(2):
         hfin[pl.ds(0, hot_dev), pl.ds(h * 128, 128)] = hotf[h]
     gacc[...] = jnp.dot(hsel[...], hfin[...].astype(bf16), preferred_element_type=f32)
-
-    def update(cc, yy):
-        at = pl.ds(pl.multiple_of((cc * NY + yy) * blk, blk), blk)
-        g = total[cc, yy].astype(f32) + gacc[at, :]
-        new_sum = sum_col[at, :] + jnp.sum(g * g, axis=1, keepdims=True) * (1.0 / width)
-        sum_col[at, :] = new_sum
-        table_out[at, :] = table_v[at, :] - g * (learning_rate / jnp.sqrt(new_sum))
-
-    update(c, y)
-
-    def gather(k):
-        ys = (y + k) % NY
-        to_y(ys, ys).wait_recv()
-        to_core(c, ys).start()
-        update(c, ys)
-
-    over(1, NY, gather)
-
-    def gather_core(k):
-        ys = (y + k) % NY
-        to_core(1 - c, ys).wait_recv()
-        update(1 - c, ys)
-
-    over(0, NY, gather_core)
+    over(0, subs // 2, lambda b: update(c, b))
+
+    def gather_update(b):
+        gather(b)
+        update(c, b)
+
+    over(subs // 2, subs, gather_update)
+
+    def gather_core(b):
+        over(0, NY, lambda k: to_core(1 - c, b, k).wait_recv())
+        update(1 - c, b)
+
+    over(0, subs, gather_core)
     for b in range(rows // 128):
         sum_out[pl.ds(b, 1), :] = jnp.sum(
             jnp.where(eye(128, 128), sum_col[pl.ds(b * 128, 128), :], 0.0), axis=0, keepdims=True
         )
+
+    for cc in range(2):
+        over(0, subs, lambda b: leave(cc, b).wait())
 
     def finish_table(k):
         p = peer(k, x, z)
@@ -487,28 +525,26 @@
         yt = (y + k) % NY
         for q in range(parts):
             y_copy(y, yt, q).wait_send()
-        g_y(y, yt).wait_send()
-        to_y(y, yt).wait_send()
+
+        def left(b):
+            g_y(b, y, yt).wait_send()
+            to_y(b, y, yt).wait_send()
+
+        over(0, subs, left)
 
     over(1, NY, finish_y)
     over(1, 2 * NY, lambda k: h_copy(dp, (dp + k) % (2 * NY)).wait_send())
 
-    def finish_core(yt):
-        g_core(yt).wait_send()
-        to_core(c, yt).wait_send()
-
-    over(0, NY, finish_core)
-
-
-def emit_kernel(table_ref, sum_ref, table_out, sum_out, sems):
-    copies = [
-        pltpu.make_async_copy(table_ref, table_out, sems.at[0]),
-        pltpu.make_async_copy(sum_ref, sum_out, sems.at[1]),
-    ]
-    for copy in copies:
-        copy.start()
-    for copy in copies:
-        copy.wait()
+    def finish_core(k):
+        g_core(k // NY, k % NY).wait_send()
+        to_core(c, k // NY, k % NY).wait_send()
+
+    over(0, subs * NY, finish_core)
+
+
+def emit_kernel(table_ref, sum_ref, table_out, sum_out):
+    table_out[...] = table_ref[...]
+    sum_out[...] = sum_ref[...]
 
 
 def per_device(bag_slots, labels, cold_ids, cold_count, table, adagrad_sum, hot_ids, w_in, w_out):
@@ -523,7 +559,8 @@
     chunk = min(8, n)
     per_y = hot_dev // NY
     parts = 2 if hot_cols % 512 == 0 else 1
-    blk = rows // (2 * NY)
+    sub = 16
+    subs = rows // (2 * NY * sub)
     groups = batch // 16
     dma = pltpu.SemaphoreType.DMA
     vmem = pl.BlockSpec(memory_space=pltpu.VMEM)
@@ -535,9 +572,16 @@
             jax.ShapeDtypeStruct((rows, width), f32),
             jax.ShapeDtypeStruct((rows // 128, 128), f32),
         ),
-        in_specs=[vmem, vmem, vmem, vmem, hbm, vmem, vmem, hbm, vmem],
-        out_specs=(vmem, vmem),
+        in_specs=[hbm] * 9,
+        out_specs=(hbm, vmem),
         scratch_shapes=[
+            pltpu.VMEM((bag, batch), i32),
+            pltpu.VMEM((1, batch), f32),
+            pltpu.VMEM((n, slots), i32),
+            pltpu.VMEM((1, n), i32),
+            pltpu.VMEM((rows // 128, 128), f32),
+            pltpu.VMEM((1, hot_dev), i32),
+            pltpu.VMEM((hidden // 128, 128), bf16),
             pltpu.VMEM((rows, width), f32),
             pltpu.VMEM(w_in.shape, bf16),
             pltpu.VMEM((rows, width), bf16),
@@ -570,12 +614,14 @@
             pltpu.VMEM((rows, 128), bf16),
             pltpu.VMEM((2, hot_dev, 128), f32),
             pltpu.VMEM((1, hidden), f32),
-            pltpu.VMEM((2, NY, blk, width), bf16),
-            pltpu.VMEM((NY, blk, width), bf16),
-            pltpu.VMEM((NY, blk, width), bf16),
-            pltpu.VMEM((NY, blk, width), bf16),
-            pltpu.VMEM((2, NY, blk, width), bf16),
-            dma((2,)),
+            pltpu.VMEM((2, subs, NY, sub, width), bf16),
+            pltpu.VMEM((subs, NY, sub, width), bf16),
+            pltpu.VMEM((subs, NY, sub, width), bf16),
+            pltpu.VMEM((subs, NY, sub, width), bf16),
+            pltpu.VMEM((2, subs, NY, sub, width), bf16),
+            pltpu.VMEM((rows, width), f32),
+            dma((9,)),
+            dma((2, subs)),
             dma((n,)), dma((n,)),
             dma((NZ,)), dma((NZ,)),
             dma((NX, NZ)), dma((NX, NZ)),
@@ -585,26 +631,28 @@
             dma((NY, parts)), dma((NY, parts)),
             dma((n,)), dma((n,)),
             dma((n,)), dma((n,)),
-            dma((NY,)), dma((NY,)),
-            dma((NY,)), dma((NY,)),
-            dma((NY,)), dma((NY,)),
-            dma((NY,)), dma((NY,)),
+            dma((subs, NY)), dma((subs, NY)),
+            dma((subs, NY)), dma((subs, NY)),
+            dma((subs, NY)), dma((subs, NY)),
+            dma((subs, NY)), dma((subs, NY)),
             dma((2 * NY,)), dma((2 * NY,)),
         ],
         compiler_params=pltpu.CompilerParams(
             collective_id=0, has_side_effects=True, vmem_limit_bytes=60 << 20
         ),
     )(
+        table,
+        w_in,
         bag_slots.T,
         labels.reshape(1, batch),
         cold_ids[0],
         cold_count,
-        table,
         adagrad_sum.reshape(rows // 128, 128),
         hot_ids.reshape(1, hot_dev),
-        w_in,
         w_out.reshape(hidden // 128, 128),
     )
+    part = pl.BlockSpec((rows // 4, width), lambda i: (i, 0))
+    whole = pl.BlockSpec((rows // 128, 128), lambda i: (0, 0))
     out_table, out_sum = pl.pallas_call(
         emit_kernel,
         name="emit",
@@ -612,9 +660,9 @@
             jax.ShapeDtypeStruct((rows, width), f32),
             jax.ShapeDtypeStruct((rows // 128, 128), f32),
         ),
-        in_specs=[vmem, vmem],
-        out_specs=(hbm, hbm),
-        scratch_shapes=[dma((2,))],
+        grid=(4,),
+        in_specs=[part, whole],
+        out_specs=(part, whole),
     )(new_table, new_sum)
     return out_table, out_sum.reshape(rows)
 

time: 95.1 us -> 94 us (0.988)
  Pallas kernels: 94.3 us -> 93.1 us
    pallas_call x1, Pallas kernels: 92.1 us -> 89.8 us  [per_device(): pl.pallas_call(functools.partial(step_kernel, groups // 4, groups // 2),...]
    pallas_call x1, Pallas kernels: 2.22 us -> 3.37 us  [per_device(): pl.pallas_call(emit_kernel, name='emit', out_shape=(jax.ShapeDtypeStruct(...]
where the time goes in v4:
time: 94 us; the launch traced here: 93.8 us
  Pallas kernels  93.1 us (99%)
    pallas_call x1, Pallas kernels, per_device(): pl.pallas_call(functools.partial(step_kernel, groups // 4, groups // 2),...  89.8 us
    pallas_call x1, Pallas kernels, per_device(): pl.pallas_call(emit_kernel, name='emit', out_shape=(jax.ShapeDtypeStruct(...  3.37 us

profile of v4, /device:TPU:1, one launch (start us, length us, event | category | flops | bytes accessed | tf_op | source)
XLA Modules:
  0.0 93.8 jit_solution(15996250315022330678)
XLA Ops:
  0.6 89.8 %step.1 = (f32[1024,256]{1,0:T(8,128)}, f32[8,128]{1,0:T(8,128)}) custom-call(f32[1024,256]{1,0:T(8,128)} %table_hbm.1, bf16[256,4096]{1,0:T(8,128)(2,1)} %w_hbm.1, s32[32,512]{1,0:T(8,128)} %bitcast.7, f32[1,512]{1,0:T(1,128)} %bitcast.11, s32[32,32]{1,0:T(8,128)} %bitcast.8, s32[1,32]{1,0:T(1,128)} %count_hbm.1, f32[8,128]{1,0:T(8,128)} %bitcast.10, ...), custom_call_target="tpu_custom_call" | custom-call | tf_op jit(solution)/shard_map/step/pallas_call | solution.py:568
  90.4 3.4 %emit.1 = (f32[1024,256]{1,0:T(8,128)}, f32[8,128]{1,0:T(8,128)}) custom-call(f32[1024,256]{1,0:T(8,128)} %get-tuple-element.6.table_ref, f32[8,128]{1,0:T(8,128)} %get-tuple-element.7.sum_ref), custom_call_target="tpu_custom_call" | custom-call | tf_op jit(solution)/shard_map/emit/pallas_call | solution.py:656

commit v5 on v4

--- a/solution.py
+++ b/solution.py
@@ -24,21 +24,24 @@
     )
 
 
+def ring(a, size):
+    return lax.rem(a, size)
+
+
 def peer(k, x, z):
-    m = k // NX
-    kz = (NZ // 2 + (1 - 2 * (m % 2)) * ((m + 1) // 2)) % NZ
-    kx = (k + 1) % NX
-    return ((x + kx) % NX) * NZ + (z + kz) % NZ
+    m = lax.div(k, NX)
+    kz = NZ + NZ // 2 + (1 - 2 * lax.rem(m, 2)) * lax.div(m + 1, 2)
+    return ring(x + k + 1, NX) * NZ + ring(z + kz, NZ)
 
 
 def y_peer(k, y):
-    return (y + NY // 2 + (1 - 2 * (k % 2)) * ((k + 1) // 2)) % NY
+    return ring(y + NY + NY // 2 + (1 - 2 * lax.rem(k, 2)) * lax.div(k + 1, 2), NY)
 
 
 def place():
     dp, me = lax.axis_index("dp"), lax.axis_index("table")
-    y, c = dp // 2, dp % 2
-    x, z = me // NZ, me % NZ
+    y, c = lax.div(dp, 2), lax.rem(dp, 2)
+    x, z = lax.div(me, NZ), lax.rem(me, NZ)
     partner = y * 2 + (1 - c)
     return dp, me, y, c, x, z, partner
 
@@ -50,8 +53,8 @@
     bag_ref, labels_ref, ids_ref, count_ref, sum_ref, hot_ids_ref, w_out_ref,
     table_v, w_v, tb, ids3, asked, flat, hot_pad, bag_rows, bag2, sum_col,
     hot, fetched, oh, served, inc, wm, acc, dpool,
-    hot_g, cold_g, hcore, hsum, hy, hz, ht, ret, oht, gacc, hfin, hsel, hotf, w_row, gl, gcore, gsum, gy, total, new_rows,
-    in_s, out_s, ids_s, ids_r, za_s, za_r, xb_s, xb_r, cc_s, cc_r, f_s, f_r,
+    hot_g, cold_g, hcore, hsum, hy, hz, ht, ret, oht, gacc, hfin, hsel, hotf, w_row, live, gl, gcore, gsum, gy, total,
+    in_s, ids_s, ids_r, za_s, za_r, xb_s, xb_r, cc_s, cc_r, f_s, f_r,
     hc_s, hc_r, hy_s, hy_r, ht_s, ht_r, c_s, c_r, gc_s, gc_r, gy_s, gy_r, ag_s, ag_r, ac_s, ac_r, ha_s, ha_r,
 ):
     n = NX * NZ
@@ -76,6 +79,9 @@
 
         lax.fori_loop(lo, hi, run, 0, unroll=unroll)
 
+    def other(k):
+        return ring(me + 1 + k, n)
+
     def eye(a, b, shift=0):
         return lax.broadcasted_iota(i32, (a, b), 0) + shift == lax.broadcasted_iota(i32, (a, b), 1)
 
@@ -86,7 +92,7 @@
     over(0, n - 1, lambda k: pl.semaphore_signal(
         barrier, inc=1, device_id=(dp, peer(k, x, z)), device_id_type=MESH))
     over(1, 2 * NY, lambda k: pl.semaphore_signal(
-        barrier, inc=1, device_id=((dp + k) % (2 * NY), me), device_id_type=MESH))
+        barrier, inc=1, device_id=(ring(dp + k, 2 * NY), me), device_id_type=MESH))
 
     small = (
         (ids_hbm, ids_ref), (hot_ids_hbm, hot_ids_ref), (bag_hbm, bag_ref), (w_out_hbm, w_out_ref),
@@ -111,6 +117,9 @@
     hot_pad[:, pl.ds(0, hot_dev)] = hot_ids_ref[...]
     for k in range(w_out_ref.shape[0]):
         w_row[:, pl.ds(k * 128, 128)] = w_out_ref[pl.ds(k, 1), :].astype(f32)
+    lane = lax.broadcasted_iota(i32, (1, slots), 1)
+    for t in range(n):
+        live[:, pl.ds(t * slots, slots)] = (lane < count_ref[:, t : t + 1]).astype(f32)
     bag = bag_ref.shape[0]
     bag_rows[...] = bag_ref[...].T
     for s in range(8):
@@ -135,6 +144,8 @@
         at = pl.ds(pl.multiple_of(16 * i, 16), 16)
         for k in range(tiles):
             t = jnp.concatenate([outs[0][8 * k : 8 * k + 8], outs[1][8 * k : 8 * k + 8]], axis=0)
+            if k * 128 >= hot_cols:
+                t = t * live[:, pl.ds(k * 128 - hot_cols, 128)]
             inc[at, pl.ds(k * 128, 128)] = t.astype(bf16)
 
     load_table.wait()
@@ -154,11 +165,11 @@
 
     def hot_to_x(zs, xo):
         blk_ = hot.at[x, zs, c]
-        remote(blk_, blk_, xb_s.at[xo, zs], xb_r.at[x, zs], dp, ((x + xo) % NX) * NZ + z).start()
+        remote(blk_, blk_, xb_s.at[xo, zs], xb_r.at[x, zs], dp, (ring(x + xo, NX)) * NZ + z).start()
 
     def hot_to_z(zo):
         blk_ = hot.at[x, z, c]
-        remote(blk_, blk_, za_s.at[zo], za_r.at[z], dp, x * NZ + (z + zo) % NZ).start()
+        remote(blk_, blk_, za_s.at[zo], za_r.at[z], dp, x * NZ + ring(z + zo, NZ)).start()
 
     over(1, NZ, hot_to_z)
     for xo in range(1, NX):
@@ -166,7 +177,7 @@
     over(pre, mid, build)
 
     def forward_x(zo):
-        zs = (z + zo) % NZ
+        zs = ring(z + zo, NZ)
         blk_ = hot.at[x, zs, c]
         remote(blk_, blk_, za_s.at[zo], za_r.at[zs], dp, me).wait_recv()
         for xo in range(1, NX):
@@ -182,7 +193,7 @@
     def serve(ch):
         for j in range(chunk):
             k = ch * chunk + j
-            p = peer((2 * n - 2 - k) % n, x, z)
+            p = peer(ring(2 * n - 2 - k, n), x, z)
 
             def arrived():
                 remote(ids3.at[p], asked.at[p], ids_s.at[p], ids_r.at[p], dp, p).wait_recv()
@@ -197,7 +208,7 @@
         served[ch] = jnp.dot(oh[...], tb[...], preferred_element_type=f32).astype(bf16)
         for j in range(chunk):
             k = ch * chunk + j
-            p = peer((2 * n - 2 - k) % n, x, z)
+            p = peer(ring(2 * n - 2 - k, n), x, z)
             block = served.at[ch, pl.ds(j * slots, slots)]
 
             def send():
@@ -216,7 +227,7 @@
     over(mid, batch // 16, build)
 
     def line_to_partner(xo):
-        xs = (x + xo) % NX
+        xs = ring(x + xo, NX)
 
         def landed(zs):
             blk_ = hot.at[xs, zs, c]
@@ -243,17 +254,10 @@
     )
 
     def fetched_wait(k):
-        p = peer(k, x, z)
+        p = other(k)
         remote(fetched.at[p], fetched.at[p], f_s.at[p], f_r.at[p], dp, p).wait_recv()
 
     over(0, n - 1, fetched_wait)
-    slot_ids = lax.broadcasted_iota(i32, (slots, width), 0)
-
-    def live(t):
-        return slot_ids < count_ref[:, t : t + 1]
-
-    for t in range(n):
-        fetched[t] = jnp.where(live(t), fetched[t].astype(f32), 0.0).astype(bf16)
     pooled = (
         acc[...]
         + jnp.dot(
@@ -308,7 +312,7 @@
         g = slot_grad(hot_cols + k * cold_step, cold_step)
         for i in range(cold_step // slots):
             t = k * (cold_step // slots) + i
-            cold_g[t] = jnp.where(live(t), g[i * slots : (i + 1) * slots], 0.0).astype(bf16)
+            cold_g[t] = g[i * slots : (i + 1) * slots].astype(bf16)
 
     def cold_send(k):
         p = peer(k, x, z)
@@ -349,8 +353,32 @@
     hsel[...] = (lax.broadcasted_iota(i32, (rows, 128), 0) == hot_pad[...]).astype(f32).astype(bf16)
     hfin[...] = jnp.zeros_like(hfin)
 
+    def finish_fetch(k):
+        p = other(k)
+        remote(ids3.at[p], asked.at[me], ids_s.at[p], ids_r.at[me], dp, p).wait_send()
+        remote(served.at[0, pl.ds(0, slots)], fetched.at[me], f_s.at[p], f_r.at[me], dp, p).wait_send()
+
+    over(0, n - 1, finish_fetch)
+
+    def finish_hot(zo):
+        blk_ = hot.at[x, z, c]
+
+        @pl.when(zo > 0)
+        def _():
+            remote(blk_, blk_, za_s.at[zo], za_r.at[z], dp, me).wait_send()
+
+        for xo in range(1, NX):
+            remote(blk_, blk_, xb_s.at[xo, zo], xb_r.at[x, zo], dp, me).wait_send()
+
+    over(0, NZ, finish_hot)
+
+    def finish_line(xs):
+        line = hot.at[xs, :, c]
+        remote(line, line, cc_s.at[xs], cc_r.at[xs], partner, me).wait_send()
+
+    over(0, NX, finish_line)
     def cold_wait(k):
-        p = peer(k, x, z)
+        p = other(k)
         to = ret.at[pl.ds(pl.multiple_of(p * slots, slots), slots)]
         remote(cold_g.at[p], to, c_s.at[p], c_r.at[p], dp, p).wait_recv()
 
@@ -373,14 +401,14 @@
 
     for i in range(pieces):
         piece_grad(1 - c, i)
-        over(0, per * NY, lambda k: g_core(i * per + k // NY, y_peer(k % NY, y)).start())
+        over(0, per * NY, lambda k: g_core(i * per + lax.div(k, NY), y_peer(ring(k, NY), y)).start())
 
     def g_send(k):
-        b, yt = k // NY, y_peer(k % NY, y)
+        b, yt = lax.div(k, NY), y_peer(ring(k, NY), y)
         g_core(b, yt).wait_recv()
         gsum[b, yt] = (gl[c, b, yt].astype(f32) + gcore[b, yt].astype(f32)).astype(bf16)
 
-        @pl.when(k % NY < NY - 1)
+        @pl.when(ring(k, NY) < NY - 1)
         def _():
             g_y(b, y, yt).start()
 
@@ -389,7 +417,7 @@
         over(i * per * NY, (i + 1) * per * NY, g_send)
 
     def y_wait(k):
-        ys = (y + k) % NY
+        ys = ring(y + k, NY)
         for q in range(parts):
             y_copy(ys, ys, q).wait_recv()
 
@@ -416,7 +444,7 @@
         return remote(part, part, ac_s.at[b, yt], ac_r.at[b, yt], partner, me)
 
     def dp_sum(b):
-        over(1, NY, lambda k: g_y(b, (y + k) % NY, (y + k) % NY).wait_recv())
+        over(1, NY, lambda k: g_y(b, ring(y + k, NY), ring(y + k, NY)).wait_recv())
         gy[b, y] = gsum[b, y]
         tot = gy[b, 0].astype(f32)
         for k in range(1, NY):
@@ -428,25 +456,21 @@
     over(0, subs, dp_sum)
 
     def t_wait(k):
-        p = peer(k, x, z)
+        p = other(k)
         remote(hz.at[p], ht.at[p], ht_s.at[p], ht_r.at[p], dp, p).wait_recv()
 
     over(0, n - 1, t_wait)
     hotf[c, pl.ds(pl.multiple_of(y * per_y, 8), per_y), :] = jnp.sum(ht[...].astype(f32), axis=0)
 
     def h_copy(src, to):
-        b = hotf.at[src % 2, pl.ds(pl.multiple_of(src // 2 * per_y, 8), per_y)]
+        b = hotf.at[lax.rem(src, 2), pl.ds(pl.multiple_of(lax.div(src, 2) * per_y, 8), per_y)]
         return remote(b, b, ha_s.at[to], ha_r.at[src], to, me)
 
-    over(1, 2 * NY, lambda k: h_copy(dp, (dp + k) % (2 * NY)).start())
+    over(1, 2 * NY, lambda k: h_copy(dp, ring(dp + k, 2 * NY)).start())
 
     def h_wait(k):
-        src = (dp + k) % (2 * NY)
+        src = ring(dp + k, 2 * NY)
         h_copy(src, src).wait_recv()
-
-    def leave(cc, b):
-        at = pl.ds(pl.multiple_of((cc * subs + b) * NY * sub, NY * sub), NY * sub)
-        return pltpu.make_async_copy(new_rows.at[at], table_out.at[at], out_s.at[cc, b])
 
     def update(cc, b):
         tall = NY * sub
@@ -454,18 +478,34 @@
         g = total[cc, b].astype(f32).reshape(tall, width) + gacc[at, :]
         new_sum = sum_col[at, :] + jnp.sum(g * g, axis=1, keepdims=True) * (1.0 / width)
         sum_col[at, :] = new_sum
-        new_rows[at, :] = table_v[at, :] - g * (learning_rate / jnp.sqrt(new_sum))
-        leave(cc, b).start()
+        table_out[at, :] = table_v[at, :] - g * (learning_rate / jnp.sqrt(new_sum))
 
     def gather(b):
         def landed(k):
-            ys = (y + k) % NY
+            ys = ring(y + k, NY)
             to_y(b, ys, ys).wait_recv()
             to_core(c, b, ys).start()
 
         over(1, NY, landed)
 
+    def finish_table(k):
+        p = other(k)
+        to = ret.at[pl.ds(pl.multiple_of(me * slots, slots), slots)]
+        remote(cold_g.at[p], to, c_s.at[p], c_r.at[me], dp, p).wait_send()
+        remote(hz.at[p], ht.at[me], ht_s.at[p], ht_r.at[me], dp, p).wait_send()
+
+    def finish_sums(k):
+        yt = ring(y + k, NY)
+        for q in range(parts):
+            y_copy(y, yt, q).wait_send()
+        over(0, subs, lambda b: g_y(b, y, yt).wait_send())
+
     over(0, subs // 2, gather)
+    over(0, n - 1, finish_table)
+    over(1, NY, finish_sums)
+    for q in range(parts):
+        core_copy(q).wait_send()
+    over(0, subs * NY, lambda k: g_core(lax.div(k, NY), ring(k, NY)).wait_send())
     over(1, 2 * NY, h_wait)
     for h in range(2):
         hfin[pl.ds(0, hot_dev), pl.ds(h * 128, 128)] = hotf[h]
@@ -488,63 +528,24 @@
             jnp.where(eye(128, 128), sum_col[pl.ds(b * 128, 128), :], 0.0), axis=0, keepdims=True
         )
 
-    for cc in range(2):
-        over(0, subs, lambda b: leave(cc, b).wait())
-
-    def finish_table(k):
-        p = peer(k, x, z)
-        remote(ids3.at[p], asked.at[me], ids_s.at[p], ids_r.at[me], dp, p).wait_send()
-        remote(served.at[0, pl.ds(0, slots)], fetched.at[me], f_s.at[p], f_r.at[me], dp, p).wait_send()
-        to = ret.at[pl.ds(pl.multiple_of(me * slots, slots), slots)]
-        remote(cold_g.at[p], to, c_s.at[p], c_r.at[me], dp, p).wait_send()
-        remote(hz.at[p], ht.at[me], ht_s.at[p], ht_r.at[me], dp, p).wait_send()
-
-    over(0, n - 1, finish_table)
-
-    def finish_hot(zo):
-        blk_ = hot.at[x, z, c]
-
-        @pl.when(zo > 0)
-        def _():
-            remote(blk_, blk_, za_s.at[zo], za_r.at[z], dp, me).wait_send()
-
-        for xo in range(1, NX):
-            remote(blk_, blk_, xb_s.at[xo, zo], xb_r.at[x, zo], dp, me).wait_send()
-
-    over(0, NZ, finish_hot)
-
-    def finish_line(xs):
-        line = hot.at[xs, :, c]
-        remote(line, line, cc_s.at[xs], cc_r.at[xs], partner, me).wait_send()
-
-    over(0, NX, finish_line)
-    for q in range(parts):
-        core_copy(q).wait_send()
-
     def finish_y(k):
-        yt = (y + k) % NY
-        for q in range(parts):
-            y_copy(y, yt, q).wait_send()
-
-        def left(b):
-            g_y(b, y, yt).wait_send()
-            to_y(b, y, yt).wait_send()
-
-        over(0, subs, left)
+        yt = ring(y + k, NY)
+        over(0, subs, lambda b: to_y(b, y, yt).wait_send())
 
     over(1, NY, finish_y)
-    over(1, 2 * NY, lambda k: h_copy(dp, (dp + k) % (2 * NY)).wait_send())
-
-    def finish_core(k):
-        g_core(k // NY, k % NY).wait_send()
-        to_core(c, k // NY, k % NY).wait_send()
-
-    over(0, subs * NY, finish_core)
-
-
-def emit_kernel(table_ref, sum_ref, table_out, sum_out):
-    table_out[...] = table_ref[...]
-    sum_out[...] = sum_ref[...]
+    over(0, subs * NY, lambda k: to_core(c, lax.div(k, NY), ring(k, NY)).wait_send())
+    over(1, 2 * NY, lambda k: h_copy(dp, ring(dp + k, 2 * NY)).wait_send())
+
+
+def emit_kernel(table_ref, sum_ref, table_out, sum_out, sems):
+    copies = [
+        pltpu.make_async_copy(table_ref, table_out, sems.at[0]),
+        pltpu.make_async_copy(sum_ref, sum_out, sems.at[1]),
+    ]
+    for copy in copies:
+        copy.start()
+    for copy in copies:
+        copy.wait()
 
 
 def per_device(bag_slots, labels, cold_ids, cold_count, table, adagrad_sum, hot_ids, w_in, w_out):
@@ -564,7 +565,7 @@
     groups = batch // 16
     dma = pltpu.SemaphoreType.DMA
     vmem = pl.BlockSpec(memory_space=pltpu.VMEM)
-    hbm = pl.BlockSpec(memory_space=pl.ANY)
+    hbm = pl.BlockSpec(memory_space=pltpu.HBM)
     new_table, new_sum = pl.pallas_call(
         functools.partial(step_kernel, groups // 4, groups // 2),
         name="step",
@@ -573,7 +574,7 @@
             jax.ShapeDtypeStruct((rows // 128, 128), f32),
         ),
         in_specs=[hbm] * 9,
-        out_specs=(hbm, vmem),
+        out_specs=(vmem, vmem),
         scratch_shapes=[
             pltpu.VMEM((bag, batch), i32),
             pltpu.VMEM((1, batch), f32),
@@ -614,14 +615,13 @@
             pltpu.VMEM((rows, 128), bf16),
             pltpu.VMEM((2, hot_dev, 128), f32),
             pltpu.VMEM((1, hidden), f32),
+            pltpu.VMEM((1, n * slots), f32),
             pltpu.VMEM((2, subs, NY, sub, width), bf16),
             pltpu.VMEM((subs, NY, sub, width), bf16),
             pltpu.VMEM((subs, NY, sub, width), bf16),
             pltpu.VMEM((subs, NY, sub, width), bf16),
             pltpu.VMEM((2, subs, NY, sub, width), bf16),
-            pltpu.VMEM((rows, width), f32),
             dma((9,)),
-            dma((2, subs)),
             dma((n,)), dma((n,)),
             dma((NZ,)), dma((NZ,)),
             dma((NX, NZ)), dma((NX, NZ)),
@@ -638,9 +638,9 @@
             dma((2 * NY,)), dma((2 * NY,)),
         ],
         compiler_params=pltpu.CompilerParams(
-            collective_id=0, has_side_effects=True, vmem_limit_bytes=60 << 20
+            collective_id=0, has_side_effects=True, vmem_limit_bytes=44 << 20
         ),
-    )(
+    )(*[pltpu.with_memory_space_constraint(v, pltpu.HBM) for v in (
         table,
         w_in,
         bag_slots.T,
@@ -650,9 +650,7 @@
         adagrad_sum.reshape(rows // 128, 128),
         hot_ids.reshape(1, hot_dev),
         w_out.reshape(hidden // 128, 128),
-    )
-    part = pl.BlockSpec((rows // 4, width), lambda i: (i, 0))
-    whole = pl.BlockSpec((rows // 128, 128), lambda i: (0, 0))
+    )])
     out_table, out_sum = pl.pallas_call(
         emit_kernel,
         name="emit",
@@ -660,9 +658,10 @@
             jax.ShapeDtypeStruct((rows, width), f32),
             jax.ShapeDtypeStruct((rows // 128, 128), f32),
         ),
-        grid=(4,),
-        in_specs=[part, whole],
-        out_specs=(part, whole),
+        in_specs=[vmem, vmem],
+        out_specs=(hbm, hbm),
+        scratch_shapes=[dma((2,))],
+        compiler_params=pltpu.CompilerParams(vmem_limit_bytes=4 << 20),
     )(new_table, new_sum)
     return out_table, out_sum.reshape(rows)
 

time: 94 us -> 88.3 us (0.939)
  Pallas kernels: 93.1 us -> 87.5 us
    pallas_call x1, Pallas kernels: 89.8 us -> 86.5 us  [per_device(): pl.pallas_call(functools.partial(step_kernel, groups // 4, groups // 2),...]
    pallas_call x1, Pallas kernels: 3.37 us -> 0.99 us  [per_device(): pl.pallas_call(emit_kernel, name='emit', out_shape=(jax.ShapeDtypeStruct(...]
where the time goes in v5:
time: 88.3 us; the launch traced here: 88.1 us
  Pallas kernels  87.5 us (99%)
    pallas_call x1, Pallas kernels, per_device(): pl.pallas_call(functools.partial(step_kernel, groups // 4, groups // 2),...  86.5 us

profile of v5, /device:TPU:1, one launch (start us, length us, event | category | flops | bytes accessed | tf_op | source)
XLA Modules:
  0.0 88.1 jit_solution(6445715247742150580)
XLA Ops:
  0.6 86.5 %step.1 = (f32[1024,256]{1,0:T(8,128)S(1)}, f32[8,128]{1,0:T(8,128)S(1)}) custom-call(f32[1024,256]{1,0:T(8,128)} %table_hbm.1, bf16[256,4096]{1,0:T(8,128)(2,1)} %w_hbm.1, s32[32,512]{1,0:T(8,128)} %bitcast.7, f32[1,512]{1,0:T(1,128)} %bitcast.11, s32[32,32]{1,0:T(8,128)} %bitcast.8, s32[1,32]{1,0:T(1,128)} %count_hbm.1, f32[8,128]{1,0:T(8,128)} %bitcast.10, ...), custom_call_target="tpu_custom_call" | custom-call | tf_op jit(solution)/shard_map/step/pallas_call | solution.py:569
  87.1 1.0 %emit.1 = (f32[1024,256]{1,0:T(8,128)}, f32[8,128]{1,0:T(8,128)}) custom-call(f32[1024,256]{1,0:T(8,128)S(1)} %get-tuple-element.6.table_ref, f32[8,128]{1,0:T(8,128)S(1)} %get-tuple-element.7.sum_ref), custom_call_target="tpu_custom_call" | custom-call | tf_op jit(solution)/shard_map/emit/pallas_call | solution.py:654

commit v6 on v5

--- a/solution.py
+++ b/solution.py
@@ -183,10 +183,6 @@
         for xo in range(1, NX):
             hot_to_x(zs, xo)
 
-    over(1, NZ, forward_x)
-    line = hot.at[x, :, c]
-    remote(line, line, cc_s.at[x], cc_r.at[x], partner, me).start()
-
     request = eye(slots, 128)
     chunk = served.shape[1] // slots
 
@@ -223,7 +219,12 @@
             else:
                 send()
 
-    over(0, n // chunk, serve)
+    chunks = n // chunk
+    over(0, chunks // 2, serve)
+    over(1, NZ, forward_x)
+    line = hot.at[x, :, c]
+    remote(line, line, cc_s.at[x], cc_r.at[x], partner, me).start()
+    over(chunks // 2, chunks, serve)
     over(mid, batch // 16, build)
 
     def line_to_partner(xo):
@@ -251,6 +252,10 @@
     over(0, NX, finish_x)
     acc[...] = jnp.dot(
         inc[:, pl.ds(0, hot_cols)], hot[...].reshape(hot_cols, width), preferred_element_type=f32
+    )
+
+    lab = jnp.concatenate(
+        [to_column(eye(128, 128), labels_ref[:, pl.ds(b * 128, 128)]) for b in range(batch // 128)], axis=0
     )
 
     def fetched_wait(k):
@@ -281,9 +286,6 @@
 
     over(0, hidden_units // step, forward, unroll=4)
     logit = jnp.sum(acc[...], axis=1, keepdims=True)
-    lab = jnp.concatenate(
-        [to_column(eye(128, 128), labels_ref[:, pl.ds(b * 128, 128)]) for b in range(batch // 128)], axis=0
-    )
     dlogit = jax.nn.sigmoid(logit) - lab
     dpool[...] = jnp.zeros_like(dpool)
     deep = min(1024, hidden_units)
@@ -295,7 +297,7 @@
             dhidden, w_v[:, at], (((1,), (1,)), ((), ())), preferred_element_type=f32
         )
 
-    over(0, hidden_units // deep, backward)
+    over(0, hidden_units // deep, backward, unroll=2 if hidden_units > deep else 1)
     dpooled = dpool[...].astype(bf16)
 
     def slot_grad(at, size):
@@ -393,28 +395,24 @@
         g = jnp.dot(oht[at, :], ret[...], preferred_element_type=f32)
         gl[cc, pl.ds(i * per, per)] = g.astype(bf16).reshape(per, NY, sub, width)
 
-    def g_core(b, yt):
-        return remote(gl.at[1 - c, b, yt], gcore.at[b, yt], gc_s.at[b, yt], gc_r.at[b, yt], partner, me)
+    def g_core(b):
+        return remote(gl.at[1 - c, b], gcore.at[b], gc_s.at[b], gc_r.at[b], partner, me)
 
     def g_y(b, src, yt):
         return remote(gsum.at[b, yt], gy.at[b, src], gy_s.at[b, yt], gy_r.at[b, src], dp_of(yt), me)
 
     for i in range(pieces):
         piece_grad(1 - c, i)
-        over(0, per * NY, lambda k: g_core(i * per + lax.div(k, NY), y_peer(ring(k, NY), y)).start())
-
-    def g_send(k):
-        b, yt = lax.div(k, NY), y_peer(ring(k, NY), y)
-        g_core(b, yt).wait_recv()
-        gsum[b, yt] = (gl[c, b, yt].astype(f32) + gcore[b, yt].astype(f32)).astype(bf16)
-
-        @pl.when(ring(k, NY) < NY - 1)
-        def _():
-            g_y(b, y, yt).start()
+        over(i * per, (i + 1) * per, lambda b: g_core(b).start())
+
+    def g_send(b):
+        g_core(b).wait_recv()
+        gsum[b] = (gl[c, b].astype(f32) + gcore[b].astype(f32)).astype(bf16)
+        over(0, NY - 1, lambda k: g_y(b, y, y_peer(k, y)).start())
 
     for i in range(pieces):
         piece_grad(c, i)
-        over(i * per * NY, (i + 1) * per * NY, g_send)
+        over(i * per, (i + 1) * per, g_send)
 
     def y_wait(k):
         ys = ring(y + k, NY)
@@ -478,6 +476,10 @@
         g = total[cc, b].astype(f32).reshape(tall, width) + gacc[at, :]
         new_sum = sum_col[at, :] + jnp.sum(g * g, axis=1, keepdims=True) * (1.0 / width)
         sum_col[at, :] = new_sum
+        if tall == 128:
+            sum_out[pl.ds(cc * subs + b, 1), :] = jnp.sum(
+                jnp.where(eye(128, 128), new_sum, 0.0), axis=0, keepdims=True
+            )
         table_out[at, :] = table_v[at, :] - g * (learning_rate / jnp.sqrt(new_sum))
 
     def gather(b):
@@ -505,7 +507,7 @@
     over(1, NY, finish_sums)
     for q in range(parts):
         core_copy(q).wait_send()
-    over(0, subs * NY, lambda k: g_core(lax.div(k, NY), ring(k, NY)).wait_send())
+    over(0, subs, lambda b: g_core(b).wait_send())
     over(1, 2 * NY, h_wait)
     for h in range(2):
         hfin[pl.ds(0, hot_dev), pl.ds(h * 128, 128)] = hotf[h]
@@ -522,19 +524,21 @@
         over(0, NY, lambda k: to_core(1 - c, b, k).wait_recv())
         update(1 - c, b)
 
-    over(0, subs, gather_core)
-    for b in range(rows // 128):
-        sum_out[pl.ds(b, 1), :] = jnp.sum(
-            jnp.where(eye(128, 128), sum_col[pl.ds(b * 128, 128), :], 0.0), axis=0, keepdims=True
-        )
+    over(0, subs - 1, gather_core)
 
     def finish_y(k):
         yt = ring(y + k, NY)
         over(0, subs, lambda b: to_y(b, y, yt).wait_send())
 
     over(1, NY, finish_y)
+    over(1, 2 * NY, lambda k: h_copy(dp, ring(dp + k, 2 * NY)).wait_send())
     over(0, subs * NY, lambda k: to_core(c, lax.div(k, NY), ring(k, NY)).wait_send())
-    over(1, 2 * NY, lambda k: h_copy(dp, ring(dp + k, 2 * NY)).wait_send())
+    gather_core(subs - 1)
+    if NY * sub != 128:
+        for b in range(rows // 128):
+            sum_out[pl.ds(b, 1), :] = jnp.sum(
+                jnp.where(eye(128, 128), sum_col[pl.ds(b * 128, 128), :], 0.0), axis=0, keepdims=True
+            )
 
 
 def emit_kernel(table_ref, sum_ref, table_out, sum_out, sems):
@@ -631,7 +635,7 @@
             dma((NY, parts)), dma((NY, parts)),
             dma((n,)), dma((n,)),
             dma((n,)), dma((n,)),
-            dma((subs, NY)), dma((subs, NY)),
+            dma((subs,)), dma((subs,)),
             dma((subs, NY)), dma((subs, NY)),
             dma((subs, NY)), dma((subs, NY)),
             dma((subs, NY)), dma((subs, NY)),

time: 88.3 us -> 85.8 us (0.972)
  Pallas kernels: 87.5 us -> 84.9 us
    pallas_call x1, Pallas kernels: 86.5 us -> 84 us  [per_device(): pl.pallas_call(functools.partial(step_kernel, groups // 4, groups // 2),...]
where the time goes in v6:
time: 85.8 us; the launch traced here: 85.6 us
  Pallas kernels  84.9 us (99%)
    pallas_call x1, Pallas kernels, per_device(): pl.pallas_call(functools.partial(step_kernel, groups // 4, groups // 2),...  84 us

profile of v6, /device:TPU:1, one launch (start us, length us, event | category | flops | bytes accessed | tf_op | source)
XLA Modules:
  0.0 85.6 jit_solution(17335740078834489145)
XLA Ops:
  0.6 84.0 %step.1 = (f32[1024,256]{1,0:T(8,128)S(1)}, f32[8,128]{1,0:T(8,128)S(1)}) custom-call(f32[1024,256]{1,0:T(8,128)} %table_hbm.1, bf16[256,4096]{1,0:T(8,128)(2,1)} %w_hbm.1, s32[32,512]{1,0:T(8,128)} %bitcast.7, f32[1,512]{1,0:T(1,128)} %bitcast.11, s32[32,32]{1,0:T(8,128)} %bitcast.8, s32[1,32]{1,0:T(1,128)} %count_hbm.1, f32[8,128]{1,0:T(8,128)} %bitcast.10, ...), custom_call_target="tpu_custom_call" | custom-call | tf_op jit(solution)/shard_map/step/pallas_call | solution.py:573
  84.6 1.0 %emit.1 = (f32[1024,256]{1,0:T(8,128)}, f32[8,128]{1,0:T(8,128)}) custom-call(f32[1024,256]{1,0:T(8,128)S(1)} %get-tuple-element.6.table_ref, f32[8,128]{1,0:T(8,128)S(1)} %get-tuple-element.7.sum_ref), custom_call_target="tpu_custom_call" | custom-call | tf_op jit(solution)/shard_map/emit/pallas_call | solution.py:658
